TPU v7x, 512 devices: a whole 4x4x16 slice. The times are simulated.
512 devices in a mesh: grid: 64 (over z, y_hi, core), orb: 8 (over y_lo, x).
Axes of the slice: x: 4, y: 4 (y_hi: 2, y_lo: 2; y = y_hi * 2 + y_lo), z: 16, core: 2. Of those that a mesh axis runs over, the one named last changes fastest.
Arguments:
- orbitals: bfloat16 [16384, 8192], P('grid', 'orb'), may hold values from -6 to 6
- points: int32 [4096], P('grid'), may hold values from 0 to 16383, as said below
Outputs:
- fitted: float32 [16384, 4096], P('grid', 'orb')
- gram: float32 [4096, 4096], P('grid', 'orb')
- density: float32 [4096], P('grid')
Inputs may be any that keep to these rules, and one draw needn't show every extreme that they name: `points`: entries 64 * g to 64 * g + 63 are distinct grid rows of slab g, the rows 256 * g to 256 * g + 255.
All inputs are finite; a program needn't handle non-finite values.
Results may differ from a plain program's by a relative error of at most 0.0003.
Values may be sent and summed in bfloat16 or wider, within the bound.
No kernel may reach another device: no remote copies, remote signals or barrier semaphores. Data moves between devices by JAX's collectives and lax.ppermute only.
A program may use at most 64 MiB of HBM per device.

v0:
```python
import jax
import jax.numpy as jnp
from jax import lax
from jax.experimental import pallas as pl
from jax.experimental.pallas import tpu as pltpu
from jax.sharding import Mesh
from jax.sharding import PartitionSpec as P

NORB = 8192
SIZES = {"zh": 4, "zl": 4, "yh": 2, "c": 2, "yl": 2, "xh": 2, "xl": 2}
AXES = tuple(SIZES)
GRID = ("zh", "zl", "yh", "c")
ORB = ("yl", "xh", "xl")
PLANE = ("yh", "c", "yl", "xh", "xl")

PARAMS = pltpu.CompilerParams(vmem_limit_bytes=20 << 20)


def routes(move):
    pairs = []
    for source in range(512):
        place, rest = {}, source
        for axis in reversed(AXES):
            place[axis] = rest % SIZES[axis]
            rest //= SIZES[axis]
        move(place)
        target = 0
        for axis in AXES:
            target = target * SIZES[axis] + place[axis]
        pairs.append((source, target))
    return pairs


def along_z(step):
    def move(place):
        z = (place["zh"] * 4 + place["zl"] + step) % 16
        place["zh"], place["zl"] = z // 4, z % 4

    return routes(move)


def flip_y(bits):
    def move(place):
        y = (place["yh"] * 2 + place["yl"]) ^ bits
        place["yh"], place["yl"] = y // 2, y % 2

    return routes(move)


def flip_core(place):
    place["c"] ^= 1


def flip_x(place):
    place["xl"] ^= 1


def sent(value, pairs):
    return lax.ppermute(value, AXES, pairs)


def contract(left, right):
    return lax.dot_general(
        left, right, (((1,), (1,)), ((), ())), preferred_element_type=jnp.float32
    )


def products_kernel(
    where, m0, m1, m2, n0, n1, n2, here, up, down, lower, upper, dens, out, sets, stage, sems
):
    zl, yh, c, yl, xl = where[0], where[1], where[2], where[3], where[4]
    planes = ((0, (here,)), (1, (up,)), (2, (lower, upper)), (3, (down,)))
    for dyl in range(2):
        for dxl in range(2):
            run = jnp.bitwise_xor(yl, dyl) * 2 + jnp.bitwise_xor(xl, dxl)
            at = 0
            for _, blocks in planes:
                for block in blocks:
                    size = block.shape[0] * 16
                    sets[dyl * 2 + dxl, at : at + size] = block[:, run].reshape(size, 1024)
                    at += size
    copies = []
    for dc, (base, faces, beside) in enumerate(((m0, m1, m2), (n0, n1, n2))):
        for dyh in range(2):
            slab = jnp.bitwise_xor(yh, dyh) * 2 + jnp.bitwise_xor(c, dc)
            turn = dc * 2 + dyh
            own = base if dyh == 0 else faces.at[1]
            both = contract(sets[0], own[...])
            both = both + contract(sets[1], beside[2 * dyh])
            both = both + contract(sets[2], faces[2 * dyh])
            both = both + contract(sets[3], beside[2 * dyh + 1])
            for dz in range(4):
                plane = lax.rem(zl + dz, 4)
                base_row = pl.multiple_of(lax.rem(plane, 2) * 32, 32)
                for zh in range(4):
                    part = both[64 * dz + 16 * zh : 64 * dz + 16 * zh + 16]
                    orb = zh * 2 + plane // 2
                    stage[turn, orb, pl.ds(base_row, 16), :] = part[:, :128]
                    stage[turn, orb, pl.ds(base_row + 16, 16), :] = part[:, 128:]
            for orb in range(8):
                stage[turn, orb, 64:72, :] = dens[...]
            copies.append(pltpu.make_async_copy(stage.at[turn], out.at[slab], sems.at[turn]))
            copies[-1].start()
    for copy in copies:
        copy.wait()


def outputs_kernel(where, points, parts, fitted, gram, density):
    scale = 1.0 / jnp.sqrt(jnp.float32(NORB))
    yh, c, gap = where[1], where[2], where[5]
    sums = []
    for y in range(2):
        for core in range(2):
            for k in range(2):
                for j in range(2):
                    sums.append(parts[y, core, k, 0, j, :64] + parts[y, core, k, 1, j, :64])
    for parity in range(2):
        for lane in range(2):
            at = 32 * parity + 16 * lane
            tall = jnp.concatenate([s[at : at + 16] for s in sums], axis=0)
            fitted[128 * lane : 128 * lane + 128, 256 * parity : 256 * parity + 256] = jnp.square(
                tall.T * scale
            )
    for r in range(64):
        gram[r : r + 1, :] = fitted[pl.ds(jnp.bitwise_and(points[r], 255), 1), :]
    shape = gram.shape
    on_diagonal = (
        lax.broadcasted_iota(jnp.int32, shape, 1) - lax.broadcasted_iota(jnp.int32, shape, 0) == gap
    )
    gram[...] = jnp.where(on_diagonal, jnp.float32(0.0), gram[...])
    total = jnp.zeros((8, 128), jnp.float32)
    for k in range(2):
        for j in range(4):
            total = total + parts[yh, c, k, j // 2, j % 2, 64:72]
    density[...] = total[0, :64] / jnp.float32(NORB)


def program(orbitals, points):
    rows, width = orbitals.shape
    mu_dev = points.shape[0]
    slab = lax.axis_index(GRID)
    local = jnp.clip(points - slab * rows, 0, rows - 1)
    chosen = jnp.take(orbitals, local, axis=0, mode="clip")
    chosen_wide = chosen.astype(jnp.float32)
    dens = jnp.sum(chosen_wide * chosen_wide, axis=1)
    dens = jnp.broadcast_to(jnp.concatenate([dens, jnp.zeros_like(dens)])[None], (8, 128))

    quarters = jnp.broadcast_to(chosen.reshape(1, 4, 16, width), (4, 4, 16, width))
    here = lax.all_to_all(
        quarters.reshape(16, 16, width),
        ("zh", "yl", "xl"),
        split_axis=0,
        concat_axis=0,
        tiled=True,
    ).reshape(4, 4, 16, width)
    side = sent(orbitals, routes(flip_x))
    f1 = sent(orbitals, flip_y(1))
    f3 = sent(orbitals, flip_y(3))
    f2 = sent(orbitals, flip_y(2))
    n0 = sent(orbitals, routes(flip_core))
    g1 = sent(side, flip_y(1))
    g3 = sent(side, flip_y(3))
    g2 = sent(side, flip_y(2))
    up = sent(here, along_z(-1))
    down = sent(here, along_z(1))
    lower = sent(here[:2], along_z(-2))
    upper = sent(here[2:], along_z(2))
    m1 = jnp.stack([f1, f2, f3])
    m2 = jnp.stack([side, g1, g2, g3])
    n1 = sent(m1, routes(flip_core))
    n2 = sent(m2, routes(flip_core))

    orb = lax.axis_index(ORB)
    where = jnp.stack(
        [lax.axis_index(a) for a in ("zl", "yh", "c", "yl", "xl")] + [slab * mu_dev - orb * 512]
    ).astype(jnp.int32)
    smem = pl.BlockSpec(memory_space=pltpu.SMEM)
    vmem = pl.BlockSpec(memory_space=pltpu.VMEM)
    blocks = pl.pallas_call(
        products_kernel,
        out_shape=jax.ShapeDtypeStruct((4, 8, 72, 128), jnp.float32),
        in_specs=[smem] + [vmem] * 12,
        out_specs=pl.BlockSpec(memory_space=pltpu.HBM),
        scratch_shapes=[
            pltpu.VMEM((4, 256, 1024), jnp.bfloat16),
            pltpu.VMEM((4, 8, 72, 128), jnp.float32),
            pltpu.SemaphoreType.DMA((4,)),
        ],
        compiler_params=PARAMS,
        name="products",
    )(where, orbitals, m1, m2, n0, n1, n2, here, up, down, lower, upper, dens)
    parts = lax.all_to_all(
        blocks.reshape(32, 72, 128), PLANE, split_axis=0, concat_axis=0, tiled=True
    ).reshape(2, 2, 2, 2, 2, 72, 128)
    return pl.pallas_call(
        outputs_kernel,
        out_shape=(
            jax.ShapeDtypeStruct((rows, 512), jnp.float32),
            jax.ShapeDtypeStruct((mu_dev, 512), jnp.float32),
            jax.ShapeDtypeStruct((mu_dev,), jnp.float32),
        ),
        in_specs=[smem, smem, vmem],
        out_specs=(vmem, vmem, vmem),
        compiler_params=PARAMS,
        name="outputs",
    )(where, points, parts)


def solution(mesh):
    torus = Mesh(mesh.devices.reshape(tuple(SIZES.values())), AXES)
    in_specs = (P(GRID, ORB), P(GRID))
    out_specs = (P(GRID, ORB), P(GRID, ORB), P(GRID))
    return jax.shard_map(
        program, mesh=torus, in_specs=in_specs, out_specs=out_specs, check_vma=False
    )
```

profile of v0, /device:TPU:1, one launch (start us, length us, event | category | flops | bytes accessed | tf_op | source)
XLA Modules:
  0.0 171.7 jit_solution(4441781727803897035)
XLA Ops:
  0.6 3.9 %collective-permute-start.3 = (bf16[256,1024]{1,0:T(8,128)(2,1)}, bf16[256,1024]{1,0:T(8,128)(2,1)S(1)}, u32[]{:S(2)}, u32[]{:S(2)}) collective-permute-start(bf16[256,1024]{1,0:T(8,128)(2,1)} %m0.1), channel_id=1, source_target_pairs={{0,1},{1,0},{2,3},{3,2},{4,5},{5,4},{6,7},{7,6},{8,9},{9,8},{10,11... | collective-permute-start | bytes 1572872 | tf_op jit(solution)/shard_map/ppermute | solution.py:59
  4.6 7.0 %collective-permute-done.3 = bf16[256,1024]{1,0:T(8,128)(2,1)S(1)} collective-permute-done((bf16[256,1024]{1,0:T(8,128)(2,1)}, bf16[256,1024]{1,0:T(8,128)(2,1)S(1)}, u32[]{:S(2)}, u32[]{:S(2)}) %collective-permute-start.3) | collective-permute-done | bytes 524320 | tf_op jit(solution)/shard_map/ppermute | solution.py:59
  11.6 9.4 %collective-permute-start.6 = (bf16[256,1024]{1,0:T(8,128)(2,1)S(1)}, bf16[256,1024]{1,0:T(8,128)(2,1)S(1)}, u32[]{:S(2)}, u32[]{:S(2)}) collective-permute-start(bf16[256,1024]{1,0:T(8,128)(2,1)S(1)} %collective-permute-done.3), channel_id=1, source_target_pairs={{0,20},{1,21},{2,22},{3,23},{4,16},{5,17},{6,18},{7,19},{8,28},{9,... | collective-permute-start | bytes 1572872 | tf_op jit(solution)/shard_map/ppermute | solution.py:59
  21.0 1.9 %collective-permute-start.2 = (bf16[256,1024]{1,0:T(8,128)(2,1)}, bf16[256,1024]{1,0:T(8,128)(2,1)}, u32[]{:S(2)}, u32[]{:S(2)}) collective-permute-start(bf16[256,1024]{1,0:T(8,128)(2,1)} %m0.1), channel_id=1, source_target_pairs={{0,20},{1,21},{2,22},{3,23},{4,16},{5,17},{6,18},{7,19},{8,28},{9,... | collective-permute-start | bytes 1572872 | tf_op jit(solution)/shard_map/ppermute | solution.py:59
  22.9 3.5 %collective-permute-start.1 = (bf16[256,1024]{1,0:T(8,128)(2,1)}, bf16[256,1024]{1,0:T(8,128)(2,1)}, u32[]{:S(2)}, u32[]{:S(2)}) collective-permute-start(bf16[256,1024]{1,0:T(8,128)(2,1)} %m0.1), channel_id=1, source_target_pairs={{0,16},{1,17},{2,18},{3,19},{4,20},{5,21},{6,22},{7,23},{8,24},{9,... | collective-permute-start | bytes 1572872 | tf_op jit(solution)/shard_map/ppermute | solution.py:59
  26.5 3.2 %collective-permute-start.5 = (bf16[256,1024]{1,0:T(8,128)(2,1)S(1)}, bf16[256,1024]{1,0:T(8,128)(2,1)S(1)}, u32[]{:S(2)}, u32[]{:S(2)}) collective-permute-start(bf16[256,1024]{1,0:T(8,128)(2,1)S(1)} %collective-permute-done.3), channel_id=1, source_target_pairs={{0,16},{1,17},{2,18},{3,19},{4,20},{5,21},{6,22},{7,23},{8,24},{9,... | collective-permute-start | bytes 1572872 | tf_op jit(solution)/shard_map/ppermute | solution.py:59
  29.8 2.2 %collective-permute-start.4 = (bf16[256,1024]{1,0:T(8,128)(2,1)S(1)}, bf16[256,1024]{1,0:T(8,128)(2,1)S(1)}, u32[]{:S(2)}, u32[]{:S(2)}) collective-permute-start(bf16[256,1024]{1,0:T(8,128)(2,1)S(1)} %collective-permute-done.3), channel_id=1, source_target_pairs={{0,4},{1,5},{2,6},{3,7},{4,0},{5,1},{6,2},{7,3},{8,12},{9,13},{10,... | collective-permute-start | bytes 1572872 | tf_op jit(solution)/shard_map/ppermute | solution.py:59
  32.6 19.8 %collective-permute-done.6 = bf16[256,1024]{1,0:T(8,128)(2,1)S(1)} collective-permute-done((bf16[256,1024]{1,0:T(8,128)(2,1)S(1)}, bf16[256,1024]{1,0:T(8,128)(2,1)S(1)}, u32[]{:S(2)}, u32[]{:S(2)}) %collective-permute-start.6) | collective-permute-done | bytes 524320 | tf_op jit(solution)/shard_map/ppermute | solution.py:59
  52.4 3.2 %collective-permute-start = (bf16[256,1024]{1,0:T(8,128)(2,1)}, bf16[256,1024]{1,0:T(8,128)(2,1)}, u32[]{:S(2)}, u32[]{:S(2)}) collective-permute-start(bf16[256,1024]{1,0:T(8,128)(2,1)} %m0.1), channel_id=1, source_target_pairs={{0,4},{1,5},{2,6},{3,7},{4,0},{5,1},{6,2},{7,3},{8,12},{9,13},{10,... | collective-permute-start | bytes 1572872 | tf_op jit(solution)/shard_map/ppermute | solution.py:59
  55.6 1.9 %gather_fusion = bf16[64,1024]{1,0:T(8,128)(2,1)S(1)} fusion(bf16[256,1024]{1,0:T(8,128)(2,1)} %m0.1, s32[1024]{0:T(1024)S(1)} %pad_clamp_fusion), kind=kCustom, calls=%fused_computation | custom fusion | bytes 262400 | tf_op jit(solution)/shard_map/jit(_take)/gather | solution.py:143
  58.4 17.2 %all-to-all-start = ((bf16[16,16,1024]{2,1,0:T(8,128)(2,1)}), bf16[16,16,1024]{2,1,0:T(8,128)(2,1)S(1)}, u32[]{:S(2)}, u32[]{:S(2)}) async-start(bf16[16,16,1024]{2,1,0:T(8,128)(2,1)} %bitcast.14), calls=%async_computation | async-start | bytes 1048576 | tf_op jit(solution)/shard_map/all_to_all | solution.py:149
  78.3 7.0 %collective-permute-start.9 = (bf16[4,256,1024]{2,1,0:T(8,128)(2,1)S(1)}, bf16[4,256,1024]{2,1,0:T(8,128)(2,1)}, u32[]{:S(2)}, u32[]{:S(2)}) collective-permute-start(bf16[4,256,1024]{2,1,0:T(8,128)(2,1)S(1)} %pad_maximum_fusion.m2), channel_id=1, source_target_pairs={{0,8},{1,9},{2,10},{3,11},{4,12},{5,13},{6,14},{7,15},{8,0},{9,1},... | collective-permute-start | bytes 6291464 | tf_op jit(solution)/shard_map/ppermute | solution.py:59
  85.3 2.7 %pad_maximum_fusion.1.m1 = bf16[3,256,1024]{2,1,0:T(8,128)(2,1)} fusion(bf16[1,256,1024]{2,1,0:T(8,128)(2,1)} %bitcast.8, bf16[1,256,1024]{2,1,0:T(8,128)(2,1)} %bitcast.7, bf16[1,256,1024]{2,1,0:T(8,128)(2,1)} %bitcast.6), kind=kLoop, calls=%fused_computation.2 | loop fusion | flops 1572864 | bytes 3145728 | tf_op jit(solution)/shard_map/stack | solution.py:168
  88.0 1.9 %collective-permute-start.8 = (bf16[3,256,1024]{2,1,0:T(8,128)(2,1)}, bf16[3,256,1024]{2,1,0:T(8,128)(2,1)}, u32[]{:S(2)}, u32[]{:S(2)}) collective-permute-start(bf16[3,256,1024]{2,1,0:T(8,128)(2,1)} %pad_maximum_fusion.1.m1), channel_id=1, source_target_pairs={{0,8},{1,9},{2,10},{3,11},{4,12},{5,13},{6,14},{7,15},{8,0},{9,1},... | collective-permute-start | bytes 4718600 | tf_op jit(solution)/shard_map/ppermute | solution.py:59
  89.9 2.4 %collective-permute-start.7 = (bf16[256,1024]{1,0:T(8,128)(2,1)S(1)}, bf16[256,1024]{1,0:T(8,128)(2,1)}, u32[]{:S(2)}, u32[]{:S(2)}) collective-permute-start(bf16[256,1024]{1,0:T(8,128)(2,1)S(1)} %copy-done), channel_id=1, source_target_pairs={{0,8},{1,9},{2,10},{3,11},{4,12},{5,13},{6,14},{7,15},{8,0},{9,1},... | collective-permute-start | bytes 1572872 | tf_op jit(solution)/shard_map/ppermute | solution.py:59
  92.3 4.5 %all-to-all-done = bf16[16,16,1024]{2,1,0:T(8,128)(2,1)S(1)} async-done(((bf16[16,16,1024]{2,1,0:T(8,128)(2,1)}), bf16[16,16,1024]{2,1,0:T(8,128)(2,1)S(1)}, u32[]{:S(2)}, u32[]{:S(2)}) %all-to-all-start) | async-done | bytes 524320 | tf_op jit(solution)/shard_map/all_to_all | solution.py:149
  96.9 11.5 %collective-permute-start.11 = (bf16[4,4,16,1024]{3,2,1,0:T(8,128)(2,1)S(1)}, bf16[4,4,16,1024]{3,2,1,0:T(8,128)(2,1)}, u32[]{:S(2)}, u32[]{:S(2)}) collective-permute-start(bf16[4,4,16,1024]{3,2,1,0:T(8,128)(2,1)S(1)} %bitcast.20), channel_id=1, source_target_pairs={{0,32},{1,33},{2,34},{3,35},{4,36},{5,37},{6,38},{7,39},{8,40},{9,... | collective-permute-start | bytes 1572872 | tf_op jit(solution)/shard_map/ppermute | solution.py:59
  108.4 2.2 %collective-permute-start.10 = (bf16[4,4,16,1024]{3,2,1,0:T(8,128)(2,1)S(1)}, bf16[4,4,16,1024]{3,2,1,0:T(8,128)(2,1)}, u32[]{:S(2)}, u32[]{:S(2)}) collective-permute-start(bf16[4,4,16,1024]{3,2,1,0:T(8,128)(2,1)S(1)} %bitcast.21), channel_id=1, source_target_pairs={{0,480},{1,481},{2,482},{3,483},{4,484},{5,485},{6,486},{7,487},{8... | collective-permute-start | bytes 1572872 | tf_op jit(solution)/shard_map/ppermute | solution.py:59
  111.4 4.5 %collective-permute-start.12 = (bf16[2,4,16,1024]{3,2,1,0:T(8,128)(2,1)}, bf16[2,4,16,1024]{3,2,1,0:T(8,128)(2,1)S(1)}, u32[]{:S(2)}, u32[]{:S(2)}) collective-permute-start(bf16[2,4,16,1024]{3,2,1,0:T(8,128)(2,1)} %bitcast.16), channel_id=1, source_target_pairs={{0,448},{1,449},{2,450},{3,451},{4,452},{5,453},{6,454},{7,455},{8... | collective-permute-start | bytes 786440 | tf_op jit(solution)/shard_map/ppermute | solution.py:59
  115.9 1.9 %collective-permute-start.13 = (bf16[2,4,16,1024]{3,2,1,0:T(8,128)(2,1)}, bf16[2,4,16,1024]{3,2,1,0:T(8,128)(2,1)}, u32[]{:S(2)}, u32[]{:S(2)}) collective-permute-start(bf16[2,4,16,1024]{3,2,1,0:T(8,128)(2,1)} %bitcast.17), channel_id=1, source_target_pairs={{0,64},{1,65},{2,66},{3,67},{4,68},{5,69},{6,70},{7,71},{8,72},{9,... | collective-permute-start | bytes 786440 | tf_op jit(solution)/shard_map/ppermute | solution.py:59
  118.0 10.3 %collective-permute-done.12.lower = bf16[2,4,16,1024]{3,2,1,0:T(8,128)(2,1)S(1)} collective-permute-done((bf16[2,4,16,1024]{3,2,1,0:T(8,128)(2,1)}, bf16[2,4,16,1024]{3,2,1,0:T(8,128)(2,1)S(1)}, u32[]{:S(2)}, u32[]{:S(2)}) %collective-permute-start.12) | collective-permute-done | bytes 262176 | tf_op jit(solution)/shard_map/ppermute | solution.py:59
  128.4 8.3 %products.1 = f32[4,8,72,128]{3,2,1,0:T(8,128)S(1)} custom-call(s32[6]{0:T(128)S(1)} %stack.54.where, bf16[256,1024]{1,0:T(8,128)(2,1)S(1)} %copy-done, bf16[3,256,1024]{2,1,0:T(8,128)(2,1)} %pad_maximum_fusion.1.m1, bf16[4,256,1024]{2,1,0:T(8,128)(2,1)S(1)} %pad_maximum_fusion.m2, bf16[256,1024]{1,0:T(8,128)(2,1)} %collective-permute-done.7.n0, ...), custom_call_target="tpu_custom_call" | custom-call | tf_op jit(solution)/shard_map/products/pallas_call | solution.py:179
  136.7 33.3 %all_to_all.10 = f32[32,72,128]{2,1,0:T(8,128)S(1)} all-to-all(f32[32,72,128]{2,1,0:T(8,128)S(1)} %bitcast.24), channel_id=1, replica_groups=mesh['zh'=4,'zl'=4,'yh'=2,'c'=2,'yl'=2,'xh'=2,'xl'=2] {'yh','c','yl','xh..., dimensions={0} | all-to-all | bytes 2359296 | tf_op jit(solution)/shard_map/all_to_all | solution.py:192
  170.0 1.7 outputs.1
  (30 shorter events, 5.2 us)
Async XLA Ops:
  0.6 11.0 %collective-permute-start.3 = (bf16[256,1024]{1,0:T(8,128)(2,1)}, bf16[256,1024]{1,0:T(8,128)(2,1)S(1)}, u32[]{:S(2)}, u32[]{:S(2)}) collective-permute-start(bf16[256,1024]{1,0:T(8,128)(2,1)} %m0.1), channel_id=1, source_target_pairs={{0,1},{1,0},{2,3},{3,2},{4,5},{5,4},{6,7},{7,6},{8,9},{9,8},{10,11... | collective-permute-start | bytes 1572872 | tf_op jit(solution)/shard_map/ppermute | solution.py:59
  11.6 40.8 %collective-permute-start.6 = (bf16[256,1024]{1,0:T(8,128)(2,1)S(1)}, bf16[256,1024]{1,0:T(8,128)(2,1)S(1)}, u32[]{:S(2)}, u32[]{:S(2)}) collective-permute-start(bf16[256,1024]{1,0:T(8,128)(2,1)S(1)} %collective-permute-done.3), channel_id=1, source_target_pairs={{0,20},{1,21},{2,22},{3,23},{4,16},{5,17},{6,18},{7,19},{8,28},{9,... | collective-permute-start | bytes 1572872 | tf_op jit(solution)/shard_map/ppermute | solution.py:59
  21.0 64.3 %collective-permute-start.2 = (bf16[256,1024]{1,0:T(8,128)(2,1)}, bf16[256,1024]{1,0:T(8,128)(2,1)}, u32[]{:S(2)}, u32[]{:S(2)}) collective-permute-start(bf16[256,1024]{1,0:T(8,128)(2,1)} %m0.1), channel_id=1, source_target_pairs={{0,20},{1,21},{2,22},{3,23},{4,16},{5,17},{6,18},{7,19},{8,28},{9,... | collective-permute-start | bytes 1572872 | tf_op jit(solution)/shard_map/ppermute | solution.py:59
  22.9 62.4 %collective-permute-start.1 = (bf16[256,1024]{1,0:T(8,128)(2,1)}, bf16[256,1024]{1,0:T(8,128)(2,1)}, u32[]{:S(2)}, u32[]{:S(2)}) collective-permute-start(bf16[256,1024]{1,0:T(8,128)(2,1)} %m0.1), channel_id=1, source_target_pairs={{0,16},{1,17},{2,18},{3,19},{4,20},{5,21},{6,22},{7,23},{8,24},{9,... | collective-permute-start | bytes 1572872 | tf_op jit(solution)/shard_map/ppermute | solution.py:59
  26.5 49.1 %collective-permute-start.5 = (bf16[256,1024]{1,0:T(8,128)(2,1)S(1)}, bf16[256,1024]{1,0:T(8,128)(2,1)S(1)}, u32[]{:S(2)}, u32[]{:S(2)}) collective-permute-start(bf16[256,1024]{1,0:T(8,128)(2,1)S(1)} %collective-permute-done.3), channel_id=1, source_target_pairs={{0,16},{1,17},{2,18},{3,19},{4,20},{5,21},{6,22},{7,23},{8,24},{9,... | collective-permute-start | bytes 1572872 | tf_op jit(solution)/shard_map/ppermute | solution.py:59
  29.8 45.9 %collective-permute-start.4 = (bf16[256,1024]{1,0:T(8,128)(2,1)S(1)}, bf16[256,1024]{1,0:T(8,128)(2,1)S(1)}, u32[]{:S(2)}, u32[]{:S(2)}) collective-permute-start(bf16[256,1024]{1,0:T(8,128)(2,1)S(1)} %collective-permute-done.3), channel_id=1, source_target_pairs={{0,4},{1,5},{2,6},{3,7},{4,0},{5,1},{6,2},{7,3},{8,12},{9,13},{10,... | collective-permute-start | bytes 1572872 | tf_op jit(solution)/shard_map/ppermute | solution.py:59
  52.4 23.3 %copy-start.2 = (bf16[256,1024]{1,0:T(8,128)(2,1)}, bf16[256,1024]{1,0:T(8,128)(2,1)S(1)}, u32[]{:S(2)}) copy-start(bf16[256,1024]{1,0:T(8,128)(2,1)S(1)} %collective-permute-done.6) | copy-start | bytes 1572868
  52.4 32.9 %collective-permute-start = (bf16[256,1024]{1,0:T(8,128)(2,1)}, bf16[256,1024]{1,0:T(8,128)(2,1)}, u32[]{:S(2)}, u32[]{:S(2)}) collective-permute-start(bf16[256,1024]{1,0:T(8,128)(2,1)} %m0.1), channel_id=1, source_target_pairs={{0,4},{1,5},{2,6},{3,7},{4,0},{5,1},{6,2},{7,3},{8,12},{9,13},{10,... | collective-permute-start | bytes 1572872 | tf_op jit(solution)/shard_map/ppermute | solution.py:59
  58.4 38.5 %all-to-all-start = ((bf16[16,16,1024]{2,1,0:T(8,128)(2,1)}), bf16[16,16,1024]{2,1,0:T(8,128)(2,1)S(1)}, u32[]{:S(2)}, u32[]{:S(2)}) async-start(bf16[16,16,1024]{2,1,0:T(8,128)(2,1)} %bitcast.14), calls=%async_computation | async-start | bytes 1048576 | tf_op jit(solution)/shard_map/all_to_all | solution.py:149
  75.6 0.8 copy-start.3
  75.6 1.0 copy-start.4
  78.2 11.7 %copy-start = (bf16[256,1024]{1,0:T(8,128)(2,1)S(1)}, bf16[256,1024]{1,0:T(8,128)(2,1)}, u32[]{:S(2)}) copy-start(bf16[256,1024]{1,0:T(8,128)(2,1)} %m0.1) | copy-start | bytes 1572868
  78.3 50.1 %collective-permute-start.9 = (bf16[4,256,1024]{2,1,0:T(8,128)(2,1)S(1)}, bf16[4,256,1024]{2,1,0:T(8,128)(2,1)}, u32[]{:S(2)}, u32[]{:S(2)}) collective-permute-start(bf16[4,256,1024]{2,1,0:T(8,128)(2,1)S(1)} %pad_maximum_fusion.m2), channel_id=1, source_target_pairs={{0,8},{1,9},{2,10},{3,11},{4,12},{5,13},{6,14},{7,15},{8,0},{9,1},... | collective-permute-start | bytes 6291464 | tf_op jit(solution)/shard_map/ppermute | solution.py:59
  88.0 27.9 %collective-permute-start.8 = (bf16[3,256,1024]{2,1,0:T(8,128)(2,1)}, bf16[3,256,1024]{2,1,0:T(8,128)(2,1)}, u32[]{:S(2)}, u32[]{:S(2)}) collective-permute-start(bf16[3,256,1024]{2,1,0:T(8,128)(2,1)} %pad_maximum_fusion.1.m1), channel_id=1, source_target_pairs={{0,8},{1,9},{2,10},{3,11},{4,12},{5,13},{6,14},{7,15},{8,0},{9,1},... | collective-permute-start | bytes 4718600 | tf_op jit(solution)/shard_map/ppermute | solution.py:59
  89.9 21.5 %collective-permute-start.7 = (bf16[256,1024]{1,0:T(8,128)(2,1)S(1)}, bf16[256,1024]{1,0:T(8,128)(2,1)}, u32[]{:S(2)}, u32[]{:S(2)}) collective-permute-start(bf16[256,1024]{1,0:T(8,128)(2,1)S(1)} %copy-done), channel_id=1, source_target_pairs={{0,8},{1,9},{2,10},{3,11},{4,12},{5,13},{6,14},{7,15},{8,0},{9,1},... | collective-permute-start | bytes 1572872 | tf_op jit(solution)/shard_map/ppermute | solution.py:59
  96.9 31.5 %collective-permute-start.11 = (bf16[4,4,16,1024]{3,2,1,0:T(8,128)(2,1)S(1)}, bf16[4,4,16,1024]{3,2,1,0:T(8,128)(2,1)}, u32[]{:S(2)}, u32[]{:S(2)}) collective-permute-start(bf16[4,4,16,1024]{3,2,1,0:T(8,128)(2,1)S(1)} %bitcast.20), channel_id=1, source_target_pairs={{0,32},{1,33},{2,34},{3,35},{4,36},{5,37},{6,38},{7,39},{8,40},{9,... | collective-permute-start | bytes 1572872 | tf_op jit(solution)/shard_map/ppermute | solution.py:59
  108.4 20.0 %collective-permute-start.10 = (bf16[4,4,16,1024]{3,2,1,0:T(8,128)(2,1)S(1)}, bf16[4,4,16,1024]{3,2,1,0:T(8,128)(2,1)}, u32[]{:S(2)}, u32[]{:S(2)}) collective-permute-start(bf16[4,4,16,1024]{3,2,1,0:T(8,128)(2,1)S(1)} %bitcast.21), channel_id=1, source_target_pairs={{0,480},{1,481},{2,482},{3,483},{4,484},{5,485},{6,486},{7,487},{8... | collective-permute-start | bytes 1572872 | tf_op jit(solution)/shard_map/ppermute | solution.py:59
  111.4 16.9 %collective-permute-start.12 = (bf16[2,4,16,1024]{3,2,1,0:T(8,128)(2,1)}, bf16[2,4,16,1024]{3,2,1,0:T(8,128)(2,1)S(1)}, u32[]{:S(2)}, u32[]{:S(2)}) collective-permute-start(bf16[2,4,16,1024]{3,2,1,0:T(8,128)(2,1)} %bitcast.16), channel_id=1, source_target_pairs={{0,448},{1,449},{2,450},{3,451},{4,452},{5,453},{6,454},{7,455},{8... | collective-permute-start | bytes 786440 | tf_op jit(solution)/shard_map/ppermute | solution.py:59
  115.9 12.5 %collective-permute-start.13 = (bf16[2,4,16,1024]{3,2,1,0:T(8,128)(2,1)}, bf16[2,4,16,1024]{3,2,1,0:T(8,128)(2,1)}, u32[]{:S(2)}, u32[]{:S(2)}) collective-permute-start(bf16[2,4,16,1024]{3,2,1,0:T(8,128)(2,1)} %bitcast.17), channel_id=1, source_target_pairs={{0,64},{1,65},{2,66},{3,67},{4,68},{5,69},{6,70},{7,71},{8,72},{9,... | collective-permute-start | bytes 786440 | tf_op jit(solution)/shard_map/ppermute | solution.py:59
  136.7 33.3 %copy-start.1 = (s32[64]{0:T(128)S(1)}, s32[64]{0:T(128)}, u32[]{:S(2)}) copy-start(s32[64]{0:T(128)} %points.1) | copy-start | bytes 772
where the time goes:
time: 172 us
  starting transfers between devices  76 us (44%)
  waiting for transfers between devices  41.7 us (24%)
  blocking collectives  33.3 us (19%)
  Pallas kernels  9.96 us (6%)
  other arithmetic  5.09 us (3%)
  local copies, waits for them, and re-layouts  4.72 us (3%)
    ppermute x14, starting transfers between devices, sent(): return lax.ppermute(value, AXES, pairs)  58.8 us
    ppermute x14, waiting for transfers between devices, sent(): return lax.ppermute(value, AXES, pairs)  37.1 us
    all_to_all x1, blocking collectives, program(): lax.all_to_all(blocks.reshape(32, 72, 128), PLANE, split_axis=0, concat_a...  33.3 us
    all_to_all x1, starting transfers between devices, program(): lax.all_to_all(quarters.reshape(16, 16, width), ('zh', 'yl', 'xl'), split...  17.2 us
    pallas_call x1, Pallas kernels, program(): pl.pallas_call(products_kernel, out_shape=jax.ShapeDtypeStruct((4, 8, 72,...  8.3 us
    all_to_all x1, waiting for transfers between devices, program(): lax.all_to_all(quarters.reshape(16, 16, width), ('zh', 'yl', 'xl'), split...  4.54 us
  transfers between devices with their start and end apart: 15, of which 4 were waited for; matrix products, arithmetic and copies ran while one was open for 5% of the time, Pallas kernels for 0%

commit v1 on v0

--- a/solution.py
+++ b/solution.py
@@ -13,7 +13,7 @@
 ORB = ("yl", "xh", "xl")
 PLANE = ("yh", "c", "yl", "xh", "xl")
 
-PARAMS = pltpu.CompilerParams(vmem_limit_bytes=20 << 20)
+PARAMS = pltpu.CompilerParams(vmem_limit_bytes=16 << 20)
 
 
 def routes(move):
@@ -65,43 +65,72 @@
     )
 
 
-def products_kernel(
-    where, m0, m1, m2, n0, n1, n2, here, up, down, lower, upper, dens, out, sets, stage, sems
-):
-    zl, yh, c, yl, xl = where[0], where[1], where[2], where[3], where[4]
-    planes = ((0, (here,)), (1, (up,)), (2, (lower, upper)), (3, (down,)))
-    for dyl in range(2):
-        for dxl in range(2):
+def pick_kernel(points, orbitals, out):
+    row = lax.broadcasted_iota(jnp.int32, (256, 64), 0)
+    hot = (row == jnp.bitwise_and(points[...], 255)).astype(jnp.bfloat16)
+    rows = lax.dot_general(
+        hot, orbitals[...], (((0,), (0,)), ((), ())), preferred_element_type=jnp.float32
+    ).astype(jnp.bfloat16)
+    for zh in range(4):
+        for k in range(4):
+            out[zh, k] = rows[16 * k : 16 * k + 16]
+
+
+def slab_products(where, turn, groups, sets, dens, stage, out, sems):
+    zl, yh, c = where[0], where[1], where[2]
+    copies = []
+    for dyh, group in enumerate(groups):
+        slab = jnp.bitwise_xor(yh, dyh) * 2 + jnp.bitwise_xor(c, turn)
+        both = None
+        for k, piece in enumerate(group):
+            part = contract(sets[k], piece[...])
+            both = part if both is None else both + part
+        for dz in range(4):
+            plane = lax.rem(zl + dz, 4)
+            base_row = pl.multiple_of(lax.rem(plane, 2) * 32, 32)
+            for zh in range(4):
+                part = both[64 * dz + 16 * zh : 64 * dz + 16 * zh + 16]
+                orb = zh * 2 + plane // 2
+                stage[dyh, orb, pl.ds(base_row, 16), :] = part[:, :128]
+                stage[dyh, orb, pl.ds(base_row + 16, 16), :] = part[:, 128:]
+        for orb in range(8):
+            stage[dyh, orb, 64:72, :] = dens[...]
+        copies.append(pltpu.make_async_copy(stage.at[dyh], out.at[slab], sems.at[dyh]))
+        copies[-1].start()
+    return copies
+
+
+def own_kernel(where, m0, m1, mf, mh, mg, here, up, down, lower, upper, dens, na, nf, nh, out, xs, kept, *scratch):
+    sets, stage, sems = scratch
+    yl, xl = where[3], where[4]
+    copies = []
+    for piece, at, size in ((na, 0, 2), (nf, 2, 3), (nh, 5, 2)):
+        copies.append(pltpu.make_async_copy(piece, xs.at[pl.ds(at, size)], sems.at[2 + at]))
+        copies[-1].start()
+    planes = ((here,), (up,), (lower, upper), (down,))
+    for dxl in range(2):
+        for dyl in range(2):
             run = jnp.bitwise_xor(yl, dyl) * 2 + jnp.bitwise_xor(xl, dxl)
             at = 0
-            for _, blocks in planes:
+            for blocks in planes:
                 for block in blocks:
                     size = block.shape[0] * 16
-                    sets[dyl * 2 + dxl, at : at + size] = block[:, run].reshape(size, 1024)
+                    sets[dxl * 2 + dyl, at : at + size] = block[:, run].reshape(size, 1024)
                     at += size
-    copies = []
-    for dc, (base, faces, beside) in enumerate(((m0, m1, m2), (n0, n1, n2))):
-        for dyh in range(2):
-            slab = jnp.bitwise_xor(yh, dyh) * 2 + jnp.bitwise_xor(c, dc)
-            turn = dc * 2 + dyh
-            own = base if dyh == 0 else faces.at[1]
-            both = contract(sets[0], own[...])
-            both = both + contract(sets[1], beside[2 * dyh])
-            both = both + contract(sets[2], faces[2 * dyh])
-            both = both + contract(sets[3], beside[2 * dyh + 1])
-            for dz in range(4):
-                plane = lax.rem(zl + dz, 4)
-                base_row = pl.multiple_of(lax.rem(plane, 2) * 32, 32)
-                for zh in range(4):
-                    part = both[64 * dz + 16 * zh : 64 * dz + 16 * zh + 16]
-                    orb = zh * 2 + plane // 2
-                    stage[turn, orb, pl.ds(base_row, 16), :] = part[:, :128]
-                    stage[turn, orb, pl.ds(base_row + 16, 16), :] = part[:, 128:]
-            for orb in range(8):
-                stage[turn, orb, 64:72, :] = dens[...]
-            copies.append(pltpu.make_async_copy(stage.at[turn], out.at[slab], sems.at[turn]))
-            copies[-1].start()
+    copies.append(pltpu.make_async_copy(sets, kept, sems.at[3]))
+    copies[-1].start()
+    groups = ((m0, mf.at[0], m1, mh.at[0]), (mf.at[1], mf.at[2], mg, mh.at[1]))
+    copies += slab_products(where, 0, groups, sets, dens, stage, out, sems)
     for copy in copies:
+        copy.wait()
+
+
+def other_kernel(where, xs, ng, kept, dens, _, out, stage, sems):
+    groups = (
+        (xs.at[0], xs.at[2], xs.at[1], xs.at[5]),
+        (xs.at[3], xs.at[4], ng, xs.at[6]),
+    )
+    for copy in slab_products(where, 1, groups, kept, dens, stage, out, sems):
         copy.wait()
 
 
@@ -139,13 +168,16 @@
     rows, width = orbitals.shape
     mu_dev = points.shape[0]
     slab = lax.axis_index(GRID)
-    local = jnp.clip(points - slab * rows, 0, rows - 1)
-    chosen = jnp.take(orbitals, local, axis=0, mode="clip")
-    chosen_wide = chosen.astype(jnp.float32)
+    quarters = pl.pallas_call(
+        pick_kernel,
+        out_shape=jax.ShapeDtypeStruct((4, 4, 16, width), orbitals.dtype),
+        compiler_params=PARAMS,
+        name="pick",
+    )(points.reshape(1, mu_dev), orbitals)
+    chosen_wide = quarters[0].reshape(mu_dev, width).astype(jnp.float32)
     dens = jnp.sum(chosen_wide * chosen_wide, axis=1)
     dens = jnp.broadcast_to(jnp.concatenate([dens, jnp.zeros_like(dens)])[None], (8, 128))
 
-    quarters = jnp.broadcast_to(chosen.reshape(1, 4, 16, width), (4, 4, 16, width))
     here = lax.all_to_all(
         quarters.reshape(16, 16, width),
         ("zh", "yl", "xl"),
@@ -154,21 +186,24 @@
         tiled=True,
     ).reshape(4, 4, 16, width)
     side = sent(orbitals, routes(flip_x))
+    f2 = sent(orbitals, flip_y(2))
     f1 = sent(orbitals, flip_y(1))
     f3 = sent(orbitals, flip_y(3))
-    f2 = sent(orbitals, flip_y(2))
-    n0 = sent(orbitals, routes(flip_core))
     g1 = sent(side, flip_y(1))
     g3 = sent(side, flip_y(3))
-    g2 = sent(side, flip_y(2))
+    mg = sent(side, flip_y(2))
+    ma = jnp.stack([orbitals, side])
+    na = sent(ma, routes(flip_core))
     up = sent(here, along_z(-1))
     down = sent(here, along_z(1))
-    lower = sent(here[:2], along_z(-2))
-    upper = sent(here[2:], along_z(2))
-    m1 = jnp.stack([f1, f2, f3])
-    m2 = jnp.stack([side, g1, g2, g3])
-    n1 = sent(m1, routes(flip_core))
-    n2 = sent(m2, routes(flip_core))
+    cuts = here[:2], here[2:]
+    lower = sent(cuts[0], along_z(-2))
+    upper = sent(cuts[1], along_z(2))
+    mf = jnp.stack([f1, f2, f3])
+    nf = sent(mf, routes(flip_core))
+    mh = jnp.stack([g1, g3])
+    nh = sent(mh, routes(flip_core))
+    ng = sent(mg, routes(flip_core))
 
     orb = lax.axis_index(ORB)
     where = jnp.stack(
@@ -176,19 +211,38 @@
     ).astype(jnp.int32)
     smem = pl.BlockSpec(memory_space=pltpu.SMEM)
     vmem = pl.BlockSpec(memory_space=pltpu.VMEM)
+    anywhere = pl.BlockSpec(memory_space=pl.ANY)
+    shape = jax.ShapeDtypeStruct((4, 8, 72, 128), jnp.float32)
+    blocks, xs, kept = pl.pallas_call(
+        own_kernel,
+        out_shape=(
+            shape,
+            jax.ShapeDtypeStruct((7, rows, width), orbitals.dtype),
+            jax.ShapeDtypeStruct((4, 256, width), orbitals.dtype),
+        ),
+        in_specs=[smem] + [vmem] * 11 + [anywhere] * 3,
+        out_specs=(anywhere,) * 3,
+        scratch_shapes=[
+            pltpu.VMEM((4, 256, width), orbitals.dtype),
+            pltpu.VMEM((2, 8, 72, 128), jnp.float32),
+            pltpu.SemaphoreType.DMA((8,)),
+        ],
+        compiler_params=PARAMS,
+        name="own_products",
+    )(where, orbitals, side, mf, mh, mg, here, up, down, lower, upper, dens, na, nf, nh)
     blocks = pl.pallas_call(
-        products_kernel,
-        out_shape=jax.ShapeDtypeStruct((4, 8, 72, 128), jnp.float32),
-        in_specs=[smem] + [vmem] * 12,
-        out_specs=pl.BlockSpec(memory_space=pltpu.HBM),
+        other_kernel,
+        out_shape=shape,
+        in_specs=[smem] + [vmem] * 4 + [anywhere],
+        out_specs=anywhere,
         scratch_shapes=[
-            pltpu.VMEM((4, 256, 1024), jnp.bfloat16),
-            pltpu.VMEM((4, 8, 72, 128), jnp.float32),
-            pltpu.SemaphoreType.DMA((4,)),
+            pltpu.VMEM((2, 8, 72, 128), jnp.float32),
+            pltpu.SemaphoreType.DMA((2,)),
         ],
-        compiler_params=PARAMS,
-        name="products",
-    )(where, orbitals, m1, m2, n0, n1, n2, here, up, down, lower, upper, dens)
+        input_output_aliases={5: 0},
+        compiler_params=PARAMS,
+        name="other_products",
+    )(where, xs, ng, kept, dens, blocks)
     parts = lax.all_to_all(
         blocks.reshape(32, 72, 128), PLANE, split_axis=0, concat_axis=0, tiled=True
     ).reshape(2, 2, 2, 2, 2, 72, 128)

time: 172 us -> 140 us (0.81)
  waiting for transfers between devices: 41.7 us -> 22.1 us
  blocking collectives: 33.3 us -> 24.5 us
  starting transfers between devices: 76 us -> 71.4 us
    ppermute x14 -> x15, waiting for transfers between devices: 37.1 us -> 22.1 us  [sent(): return lax.ppermute(value, AXES, pairs)]
    all_to_all x1, blocking collectives: 33.3 us -> 24.5 us  [program(): lax.all_to_all(blocks.reshape(32, 72, 128), PLANE, split_axis=0, concat_a...]
    all_to_all x1, waiting for transfers between devices: 4.54 us -> 0.01 us  [program(): lax.all_to_all(quarters.reshape(16, 16, width), ('zh', 'yl', 'xl'), split...]
    all_to_all x1, starting transfers between devices: 17.2 us -> 14.9 us  [program(): lax.all_to_all(quarters.reshape(16, 16, width), ('zh', 'yl', 'xl'), split...]
    ppermute x14 -> x15, starting transfers between devices: 58.8 us -> 56.5 us  [sent(): return lax.ppermute(value, AXES, pairs)]
    gather x1 -> x0, local copies, waits for them, and re-layouts: 1.94 us -> none  [program(): chosen = jnp.take(orbitals, local, axis=0, mode='clip')]
    unnamed x10 -> x14, local copies, waits for them, and re-layouts: 1 us -> 2.8 us
    pallas_call x1 -> x3, Pallas kernels: 8.3 us -> 9.53 us  [the longest x1 4.78 us: program(): pl.pallas_call(own_kernel, out_shape=(shape, jax.ShapeDtypeStruct((7, row...]
  transfers between devices with their start and end apart: 15 -> 16, of which waited for: 4 -> 4; matrix products, arithmetic and copies ran while one was open for 5% -> 4% of each run, Pallas kernels for 0% -> 4%
where the time goes in v1:
time: 140 us; the launch traced here: 139 us
  starting transfers between devices  71.4 us (51%)
  blocking collectives  24.5 us (18%)
  waiting for transfers between devices  22.1 us (16%)
  Pallas kernels  11.2 us (8%)
  other arithmetic  4.74 us (3%)
  local copies, waits for them, and re-layouts  3.81 us (3%)
    ppermute x15, starting transfers between devices, sent(): return lax.ppermute(value, AXES, pairs)  56.5 us
    all_to_all x1, blocking collectives, program(): lax.all_to_all(blocks.reshape(32, 72, 128), PLANE, split_axis=0, concat_a...  24.5 us
    ppermute x15, waiting for transfers between devices, sent(): return lax.ppermute(value, AXES, pairs)  22.1 us
    all_to_all x1, starting transfers between devices, program(): lax.all_to_all(quarters.reshape(16, 16, width), ('zh', 'yl', 'xl'), split...  14.9 us
    pallas_call x1, Pallas kernels, program(): pl.pallas_call(own_kernel, out_shape=(shape, jax.ShapeDtypeStruct((7, row...  4.78 us
    pallas_call x1, Pallas kernels, program(): pl.pallas_call(other_kernel, out_shape=shape, in_specs=[smem] + [vmem] *...  3.71 us
    unnamed x14, local copies, waits for them, and re-layouts  2.8 us
  transfers between devices with their start and end apart: 16, of which 4 were waited for; matrix products, arithmetic and copies ran while one was open for 4% of the time, Pallas kernels for 4%

profile of v1, /device:TPU:1, one launch (start us, length us, event | category | flops | bytes accessed | tf_op | source)
XLA Modules:
  0.0 138.7 jit_solution(16389247840287161145)
XLA Ops:
  0.6 3.9 %collective-permute-start = (bf16[256,1024]{1,0:T(8,128)(2,1)}, bf16[256,1024]{1,0:T(8,128)(2,1)S(1)}, u32[]{:S(2)}, u32[]{:S(2)}) collective-permute-start(bf16[256,1024]{1,0:T(8,128)(2,1)} %m0.1), channel_id=1, source_target_pairs={{0,1},{1,0},{2,3},{3,2},{4,5},{5,4},{6,7},{7,6},{8,9},{9,8},{10,11... | collective-permute-start | bytes 1572872 | tf_op jit(solution)/shard_map/ppermute | solution.py:59
  4.6 3.2 %collective-permute-start.1 = (bf16[256,1024]{1,0:T(8,128)(2,1)}, bf16[256,1024]{1,0:T(8,128)(2,1)S(1)}, u32[]{:S(2)}, u32[]{:S(2)}) collective-permute-start(bf16[256,1024]{1,0:T(8,128)(2,1)} %m0.1), channel_id=1, source_target_pairs={{0,4},{1,5},{2,6},{3,7},{4,0},{5,1},{6,2},{7,3},{8,12},{9,13},{10,... | collective-permute-start | bytes 1572872 | tf_op jit(solution)/shard_map/ppermute | solution.py:59
  7.8 4.5 %collective-permute-start.2 = (bf16[256,1024]{1,0:T(8,128)(2,1)}, bf16[256,1024]{1,0:T(8,128)(2,1)S(1)}, u32[]{:S(2)}, u32[]{:S(2)}) collective-permute-start(bf16[256,1024]{1,0:T(8,128)(2,1)} %m0.1), channel_id=1, source_target_pairs={{0,16},{1,17},{2,18},{3,19},{4,20},{5,21},{6,22},{7,23},{8,24},{9,... | collective-permute-start | bytes 1572872 | tf_op jit(solution)/shard_map/ppermute | solution.py:59
  12.3 1.9 %collective-permute-start.3 = (bf16[256,1024]{1,0:T(8,128)(2,1)}, bf16[256,1024]{1,0:T(8,128)(2,1)S(1)}, u32[]{:S(2)}, u32[]{:S(2)}) collective-permute-start(bf16[256,1024]{1,0:T(8,128)(2,1)} %m0.1), channel_id=1, source_target_pairs={{0,20},{1,21},{2,22},{3,23},{4,16},{5,17},{6,18},{7,19},{8,28},{9,... | collective-permute-start | bytes 1572872 | tf_op jit(solution)/shard_map/ppermute | solution.py:59
  17.0 14.9 %all-to-all-start = ((bf16[16,16,1024]{2,1,0:T(8,128)(2,1)}), bf16[16,16,1024]{2,1,0:T(8,128)(2,1)S(1)}, u32[]{:S(2)}, u32[]{:S(2)}) async-start(bf16[16,16,1024]{2,1,0:T(8,128)(2,1)} %bitcast.12), calls=%async_computation | async-start | bytes 1048576 | tf_op jit(solution)/shard_map/all_to_all | solution.py:181
  31.9 5.7 %collective-permute-start.5 = (bf16[256,1024]{1,0:T(8,128)(2,1)S(1)}, bf16[256,1024]{1,0:T(8,128)(2,1)S(1)}, u32[]{:S(2)}, u32[]{:S(2)}) collective-permute-start(bf16[256,1024]{1,0:T(8,128)(2,1)S(1)} %collective-permute-done.m1), channel_id=1, source_target_pairs={{0,20},{1,21},{2,22},{3,23},{4,16},{5,17},{6,18},{7,19},{8,28},{9,... | collective-permute-start | bytes 1572872 | tf_op jit(solution)/shard_map/ppermute | solution.py:59
  37.6 1.9 %collective-permute-start.4 = (bf16[256,1024]{1,0:T(8,128)(2,1)S(1)}, bf16[256,1024]{1,0:T(8,128)(2,1)S(1)}, u32[]{:S(2)}, u32[]{:S(2)}) collective-permute-start(bf16[256,1024]{1,0:T(8,128)(2,1)S(1)} %collective-permute-done.m1), channel_id=1, source_target_pairs={{0,4},{1,5},{2,6},{3,7},{4,0},{5,1},{6,2},{7,3},{8,12},{9,13},{10,... | collective-permute-start | bytes 1572872 | tf_op jit(solution)/shard_map/ppermute | solution.py:59
  40.7 1.6 %pad_maximum_fusion.mf = bf16[3,256,1024]{2,1,0:T(8,128)(2,1)S(1)} fusion(bf16[1,256,1024]{2,1,0:T(8,128)(2,1)} %bitcast.32, bf16[1,256,1024]{2,1,0:T(8,128)(2,1)} %bitcast.30, bf16[1,256,1024]{2,1,0:T(8,128)(2,1)} %bitcast.28), kind=kLoop, calls=%fused_computation | loop fusion | flops 1572864 | bytes 3145728 | tf_op jit(solution)/shard_map/stack | solution.py:202
  42.3 5.2 %collective-permute-start.12 = (bf16[3,256,1024]{2,1,0:T(8,128)(2,1)S(1)}, bf16[3,256,1024]{2,1,0:T(8,128)(2,1)}, u32[]{:S(2)}, u32[]{:S(2)}) collective-permute-start(bf16[3,256,1024]{2,1,0:T(8,128)(2,1)S(1)} %pad_maximum_fusion.mf), channel_id=1, source_target_pairs={{0,8},{1,9},{2,10},{3,11},{4,12},{5,13},{6,14},{7,15},{8,0},{9,1},... | collective-permute-start | bytes 4718600 | tf_op jit(solution)/shard_map/ppermute | solution.py:59
  48.6 1.9 %collective-permute-start.11 = (bf16[2,256,1024]{2,1,0:T(8,128)(2,1)}, bf16[2,256,1024]{2,1,0:T(8,128)(2,1)}, u32[]{:S(2)}, u32[]{:S(2)}) collective-permute-start(bf16[2,256,1024]{2,1,0:T(8,128)(2,1)} %pad_maximum_fusion.2), channel_id=1, source_target_pairs={{0,8},{1,9},{2,10},{3,11},{4,12},{5,13},{6,14},{7,15},{8,0},{9,1},... | collective-permute-start | bytes 3145736 | tf_op jit(solution)/shard_map/ppermute | solution.py:59
  50.5 3.2 %collective-permute-done.4 = bf16[256,1024]{1,0:T(8,128)(2,1)S(1)} collective-permute-done((bf16[256,1024]{1,0:T(8,128)(2,1)S(1)}, bf16[256,1024]{1,0:T(8,128)(2,1)S(1)}, u32[]{:S(2)}, u32[]{:S(2)}) %collective-permute-start.4) | collective-permute-done | bytes 524320 | tf_op jit(solution)/shard_map/ppermute | solution.py:59
  54.8 5.2 %collective-permute-start.13 = (bf16[2,256,1024]{2,1,0:T(8,128)(2,1)}, bf16[2,256,1024]{2,1,0:T(8,128)(2,1)}, u32[]{:S(2)}, u32[]{:S(2)}) collective-permute-start(bf16[2,256,1024]{2,1,0:T(8,128)(2,1)} %pad_maximum_fusion.1.mh), channel_id=1, source_target_pairs={{0,8},{1,9},{2,10},{3,11},{4,12},{5,13},{6,14},{7,15},{8,0},{9,1},... | collective-permute-start | bytes 3145736 | tf_op jit(solution)/shard_map/ppermute | solution.py:59
  60.0 2.1 %collective-permute-start.6 = (bf16[256,1024]{1,0:T(8,128)(2,1)S(1)}, bf16[256,1024]{1,0:T(8,128)(2,1)}, u32[]{:S(2)}, u32[]{:S(2)}) collective-permute-start(bf16[256,1024]{1,0:T(8,128)(2,1)S(1)} %collective-permute-done.m1), channel_id=1, source_target_pairs={{0,16},{1,17},{2,18},{3,19},{4,20},{5,21},{6,22},{7,23},{8,24},{9,... | collective-permute-start | bytes 1572872 | tf_op jit(solution)/shard_map/ppermute | solution.py:59
  62.1 6.4 %collective-permute-start.7 = (bf16[4,4,16,1024]{3,2,1,0:T(8,128)(2,1)S(1)}, bf16[4,4,16,1024]{3,2,1,0:T(8,128)(2,1)}, u32[]{:S(2)}, u32[]{:S(2)}) collective-permute-start(bf16[4,4,16,1024]{3,2,1,0:T(8,128)(2,1)S(1)} %bitcast.20), channel_id=1, source_target_pairs={{0,480},{1,481},{2,482},{3,483},{4,484},{5,485},{6,486},{7,487},{8... | collective-permute-start | bytes 1572872 | tf_op jit(solution)/shard_map/ppermute | solution.py:59
  68.5 8.5 %collective-permute-done.6.mg = bf16[256,1024]{1,0:T(8,128)(2,1)} collective-permute-done((bf16[256,1024]{1,0:T(8,128)(2,1)S(1)}, bf16[256,1024]{1,0:T(8,128)(2,1)}, u32[]{:S(2)}, u32[]{:S(2)}) %collective-permute-start.6) | collective-permute-done | bytes 524320 | tf_op jit(solution)/shard_map/ppermute | solution.py:59
  77.0 2.4 %collective-permute-start.8 = (bf16[4,4,16,1024]{3,2,1,0:T(8,128)(2,1)S(1)}, bf16[4,4,16,1024]{3,2,1,0:T(8,128)(2,1)}, u32[]{:S(2)}, u32[]{:S(2)}) collective-permute-start(bf16[4,4,16,1024]{3,2,1,0:T(8,128)(2,1)S(1)} %bitcast.21), channel_id=1, source_target_pairs={{0,32},{1,33},{2,34},{3,35},{4,36},{5,37},{6,38},{7,39},{8,40},{9,... | collective-permute-start | bytes 1572872 | tf_op jit(solution)/shard_map/ppermute | solution.py:59
  79.4 3.0 %collective-permute-start.14 = (bf16[256,1024]{1,0:T(8,128)(2,1)}, bf16[256,1024]{1,0:T(8,128)(2,1)}, u32[]{:S(2)}, u32[]{:S(2)}) collective-permute-start(bf16[256,1024]{1,0:T(8,128)(2,1)} %collective-permute-done.6.mg), channel_id=1, source_target_pairs={{0,8},{1,9},{2,10},{3,11},{4,12},{5,13},{6,14},{7,15},{8,0},{9,1},... | collective-permute-start | bytes 1572872 | tf_op jit(solution)/shard_map/ppermute | solution.py:59
  83.2 3.4 %collective-permute-start.10 = (bf16[2,4,16,1024]{3,2,1,0:T(8,128)(2,1)}, bf16[2,4,16,1024]{3,2,1,0:T(8,128)(2,1)S(1)}, u32[]{:S(2)}, u32[]{:S(2)}) collective-permute-start(bf16[2,4,16,1024]{3,2,1,0:T(8,128)(2,1)} %bitcast.15), channel_id=1, source_target_pairs={{0,64},{1,65},{2,66},{3,67},{4,68},{5,69},{6,70},{7,71},{8,72},{9,... | collective-permute-start | bytes 786440 | tf_op jit(solution)/shard_map/ppermute | solution.py:59
  86.6 5.8 %collective-permute-start.9 = (bf16[2,4,16,1024]{3,2,1,0:T(8,128)(2,1)}, bf16[2,4,16,1024]{3,2,1,0:T(8,128)(2,1)}, u32[]{:S(2)}, u32[]{:S(2)}) collective-permute-start(bf16[2,4,16,1024]{3,2,1,0:T(8,128)(2,1)} %bitcast.14), channel_id=1, source_target_pairs={{0,448},{1,449},{2,450},{3,451},{4,452},{5,453},{6,454},{7,455},{8... | collective-permute-start | bytes 786440 | tf_op jit(solution)/shard_map/ppermute | solution.py:59
  93.7 9.8 %collective-permute-done.10.upper = bf16[2,4,16,1024]{3,2,1,0:T(8,128)(2,1)S(1)} collective-permute-done((bf16[2,4,16,1024]{3,2,1,0:T(8,128)(2,1)}, bf16[2,4,16,1024]{3,2,1,0:T(8,128)(2,1)S(1)}, u32[]{:S(2)}, u32[]{:S(2)}) %collective-permute-start.10) | collective-permute-done | bytes 262176 | tf_op jit(solution)/shard_map/ppermute | solution.py:59
  104.0 4.8 %own_products.1 = (f32[4,8,72,128]{3,2,1,0:T(8,128)S(1)}, bf16[7,256,1024]{2,1,0:T(8,128)(2,1)S(1)}, bf16[4,256,1024]{2,1,0:T(8,128)(2,1)S(1)}) custom-call(s32[6]{0:T(128)S(1)} %stack.57.where, bf16[256,1024]{1,0:T(8,128)(2,1)S(1)} %copy-done.1, bf16[256,1024]{1,0:T(8,128)(2,1)S(1)} %collective-permute-done.m1, ...), custom_call_target="tpu_custom_call" | custom-call | tf_op jit(solution)/shard_map/own_products/pallas_call | solution.py:216
  108.8 3.7 %other_products.1 = f32[4,8,72,128]{3,2,1,0:T(8,128)S(1)} custom-call(s32[6]{0:T(128)S(1)} %stack.57.where, bf16[7,256,1024]{2,1,0:T(8,128)(2,1)S(1)} %get-tuple-element.6.xs, bf16[256,1024]{1,0:T(8,128)(2,1)} %collective-permute-done.14.ng, bf16[4,256,1024]{2,1,0:T(8,128)(2,1)S(1)} %get-tuple-element.7.kept, ...), custom_call_target="tpu_custom_call", output_to_operand_aliasing={{}: (5, {})} | custom-call | tf_op jit(solution)/shard_map/other_products/pallas_call | solution.py:233
  112.6 24.5 %all_to_all.10 = f32[32,72,128]{2,1,0:T(8,128)S(1)} all-to-all(f32[32,72,128]{2,1,0:T(8,128)S(1)} %bitcast.24), channel_id=1, replica_groups=mesh['zh'=4,'zl'=4,'yh'=2,'c'=2,'yl'=2,'xh'=2,'xl'=2] {'yh','c','yl','xh..., dimensions={0} | all-to-all | bytes 2359296 | tf_op jit(solution)/shard_map/all_to_all | solution.py:246
  137.1 1.7 %outputs.1 = (f32[256,512]{1,0:T(8,128)}, f32[64,512]{1,0:T(8,128)}, f32[64]{0:T(128)}) custom-call(s32[6]{0:T(128)S(1)} %stack.57.where, s32[64]{0:T(128)S(1)} %copy-done.3, f32[2,2,2,2,2,72,128]{6,5,4,3,2,1,0:T(8,128)S(1)} %bitcast.23), custom_call_target="tpu_custom_call" | custom-call | tf_op jit(solution)/shard_map/outputs/pallas_call | solution.py:249
  (36 shorter events, 8.5 us)
Async XLA Ops:
  0.6 31.3 %collective-permute-start = (bf16[256,1024]{1,0:T(8,128)(2,1)}, bf16[256,1024]{1,0:T(8,128)(2,1)S(1)}, u32[]{:S(2)}, u32[]{:S(2)}) collective-permute-start(bf16[256,1024]{1,0:T(8,128)(2,1)} %m0.1), channel_id=1, source_target_pairs={{0,1},{1,0},{2,3},{3,2},{4,5},{5,4},{6,7},{7,6},{8,9},{9,8},{10,11... | collective-permute-start | bytes 1572872 | tf_op jit(solution)/shard_map/ppermute | solution.py:59
  4.6 35.0 %collective-permute-start.1 = (bf16[256,1024]{1,0:T(8,128)(2,1)}, bf16[256,1024]{1,0:T(8,128)(2,1)S(1)}, u32[]{:S(2)}, u32[]{:S(2)}) collective-permute-start(bf16[256,1024]{1,0:T(8,128)(2,1)} %m0.1), channel_id=1, source_target_pairs={{0,4},{1,5},{2,6},{3,7},{4,0},{5,1},{6,2},{7,3},{8,12},{9,13},{10,... | collective-permute-start | bytes 1572872 | tf_op jit(solution)/shard_map/ppermute | solution.py:59
  7.8 31.8 %collective-permute-start.2 = (bf16[256,1024]{1,0:T(8,128)(2,1)}, bf16[256,1024]{1,0:T(8,128)(2,1)S(1)}, u32[]{:S(2)}, u32[]{:S(2)}) collective-permute-start(bf16[256,1024]{1,0:T(8,128)(2,1)} %m0.1), channel_id=1, source_target_pairs={{0,16},{1,17},{2,18},{3,19},{4,20},{5,21},{6,22},{7,23},{8,24},{9,... | collective-permute-start | bytes 1572872 | tf_op jit(solution)/shard_map/ppermute | solution.py:59
  12.3 27.2 %collective-permute-start.3 = (bf16[256,1024]{1,0:T(8,128)(2,1)}, bf16[256,1024]{1,0:T(8,128)(2,1)S(1)}, u32[]{:S(2)}, u32[]{:S(2)}) collective-permute-start(bf16[256,1024]{1,0:T(8,128)(2,1)} %m0.1), channel_id=1, source_target_pairs={{0,20},{1,21},{2,22},{3,23},{4,16},{5,17},{6,18},{7,19},{8,28},{9,... | collective-permute-start | bytes 1572872 | tf_op jit(solution)/shard_map/ppermute | solution.py:59
  14.3 1.1 copy-start
  15.3 0.7 copy-start.2
  17.0 45.1 %all-to-all-start = ((bf16[16,16,1024]{2,1,0:T(8,128)(2,1)}), bf16[16,16,1024]{2,1,0:T(8,128)(2,1)S(1)}, u32[]{:S(2)}, u32[]{:S(2)}) async-start(bf16[16,16,1024]{2,1,0:T(8,128)(2,1)} %bitcast.12), calls=%async_computation | async-start | bytes 1048576 | tf_op jit(solution)/shard_map/all_to_all | solution.py:181
  31.9 18.6 %collective-permute-start.5 = (bf16[256,1024]{1,0:T(8,128)(2,1)S(1)}, bf16[256,1024]{1,0:T(8,128)(2,1)S(1)}, u32[]{:S(2)}, u32[]{:S(2)}) collective-permute-start(bf16[256,1024]{1,0:T(8,128)(2,1)S(1)} %collective-permute-done.m1), channel_id=1, source_target_pairs={{0,20},{1,21},{2,22},{3,23},{4,16},{5,17},{6,18},{7,19},{8,28},{9,... | collective-permute-start | bytes 1572872 | tf_op jit(solution)/shard_map/ppermute | solution.py:59
  37.6 16.2 %collective-permute-start.4 = (bf16[256,1024]{1,0:T(8,128)(2,1)S(1)}, bf16[256,1024]{1,0:T(8,128)(2,1)S(1)}, u32[]{:S(2)}, u32[]{:S(2)}) collective-permute-start(bf16[256,1024]{1,0:T(8,128)(2,1)S(1)} %collective-permute-done.m1), channel_id=1, source_target_pairs={{0,4},{1,5},{2,6},{3,7},{4,0},{5,1},{6,2},{7,3},{8,12},{9,13},{10,... | collective-permute-start | bytes 1572872 | tf_op jit(solution)/shard_map/ppermute | solution.py:59
  39.5 0.8 copy-start.4
  39.6 1.0 copy-start.5
  39.6 1.1 copy-start.6
  40.7 6.8 %copy-start.1 = (bf16[256,1024]{1,0:T(8,128)(2,1)S(1)}, bf16[256,1024]{1,0:T(8,128)(2,1)}, u32[]{:S(2)}) copy-start(bf16[256,1024]{1,0:T(8,128)(2,1)} %m0.1) | copy-start | bytes 1572868
  42.3 44.3 %collective-permute-start.12 = (bf16[3,256,1024]{2,1,0:T(8,128)(2,1)S(1)}, bf16[3,256,1024]{2,1,0:T(8,128)(2,1)}, u32[]{:S(2)}, u32[]{:S(2)}) collective-permute-start(bf16[3,256,1024]{2,1,0:T(8,128)(2,1)S(1)} %pad_maximum_fusion.mf), channel_id=1, source_target_pairs={{0,8},{1,9},{2,10},{3,11},{4,12},{5,13},{6,14},{7,15},{8,0},{9,1},... | collective-permute-start | bytes 4718600 | tf_op jit(solution)/shard_map/ppermute | solution.py:59
  48.6 30.8 %collective-permute-start.11 = (bf16[2,256,1024]{2,1,0:T(8,128)(2,1)}, bf16[2,256,1024]{2,1,0:T(8,128)(2,1)}, u32[]{:S(2)}, u32[]{:S(2)}) collective-permute-start(bf16[2,256,1024]{2,1,0:T(8,128)(2,1)} %pad_maximum_fusion.2), channel_id=1, source_target_pairs={{0,8},{1,9},{2,10},{3,11},{4,12},{5,13},{6,14},{7,15},{8,0},{9,1},... | collective-permute-start | bytes 3145736 | tf_op jit(solution)/shard_map/ppermute | solution.py:59
  54.8 28.4 %collective-permute-start.13 = (bf16[2,256,1024]{2,1,0:T(8,128)(2,1)}, bf16[2,256,1024]{2,1,0:T(8,128)(2,1)}, u32[]{:S(2)}, u32[]{:S(2)}) collective-permute-start(bf16[2,256,1024]{2,1,0:T(8,128)(2,1)} %pad_maximum_fusion.1.mh), channel_id=1, source_target_pairs={{0,8},{1,9},{2,10},{3,11},{4,12},{5,13},{6,14},{7,15},{8,0},{9,1},... | collective-permute-start | bytes 3145736 | tf_op jit(solution)/shard_map/ppermute | solution.py:59
  60.0 17.0 %collective-permute-start.6 = (bf16[256,1024]{1,0:T(8,128)(2,1)S(1)}, bf16[256,1024]{1,0:T(8,128)(2,1)}, u32[]{:S(2)}, u32[]{:S(2)}) collective-permute-start(bf16[256,1024]{1,0:T(8,128)(2,1)S(1)} %collective-permute-done.m1), channel_id=1, source_target_pairs={{0,16},{1,17},{2,18},{3,19},{4,20},{5,21},{6,22},{7,23},{8,24},{9,... | collective-permute-start | bytes 1572872 | tf_op jit(solution)/shard_map/ppermute | solution.py:59
  62.1 41.9 %collective-permute-start.7 = (bf16[4,4,16,1024]{3,2,1,0:T(8,128)(2,1)S(1)}, bf16[4,4,16,1024]{3,2,1,0:T(8,128)(2,1)}, u32[]{:S(2)}, u32[]{:S(2)}) collective-permute-start(bf16[4,4,16,1024]{3,2,1,0:T(8,128)(2,1)S(1)} %bitcast.20), channel_id=1, source_target_pairs={{0,480},{1,481},{2,482},{3,483},{4,484},{5,485},{6,486},{7,487},{8... | collective-permute-start | bytes 1572872 | tf_op jit(solution)/shard_map/ppermute | solution.py:59
  77.0 27.0 %collective-permute-start.8 = (bf16[4,4,16,1024]{3,2,1,0:T(8,128)(2,1)S(1)}, bf16[4,4,16,1024]{3,2,1,0:T(8,128)(2,1)}, u32[]{:S(2)}, u32[]{:S(2)}) collective-permute-start(bf16[4,4,16,1024]{3,2,1,0:T(8,128)(2,1)S(1)} %bitcast.21), channel_id=1, source_target_pairs={{0,32},{1,33},{2,34},{3,35},{4,36},{5,37},{6,38},{7,39},{8,40},{9,... | collective-permute-start | bytes 1572872 | tf_op jit(solution)/shard_map/ppermute | solution.py:59
  79.4 29.4 %collective-permute-start.14 = (bf16[256,1024]{1,0:T(8,128)(2,1)}, bf16[256,1024]{1,0:T(8,128)(2,1)}, u32[]{:S(2)}, u32[]{:S(2)}) collective-permute-start(bf16[256,1024]{1,0:T(8,128)(2,1)} %collective-permute-done.6.mg), channel_id=1, source_target_pairs={{0,8},{1,9},{2,10},{3,11},{4,12},{5,13},{6,14},{7,15},{8,0},{9,1},... | collective-permute-start | bytes 1572872 | tf_op jit(solution)/shard_map/ppermute | solution.py:59
  83.2 20.3 %collective-permute-start.10 = (bf16[2,4,16,1024]{3,2,1,0:T(8,128)(2,1)}, bf16[2,4,16,1024]{3,2,1,0:T(8,128)(2,1)S(1)}, u32[]{:S(2)}, u32[]{:S(2)}) collective-permute-start(bf16[2,4,16,1024]{3,2,1,0:T(8,128)(2,1)} %bitcast.15), channel_id=1, source_target_pairs={{0,64},{1,65},{2,66},{3,67},{4,68},{5,69},{6,70},{7,71},{8,72},{9,... | collective-permute-start | bytes 786440 | tf_op jit(solution)/shard_map/ppermute | solution.py:59
  86.6 17.4 %collective-permute-start.9 = (bf16[2,4,16,1024]{3,2,1,0:T(8,128)(2,1)}, bf16[2,4,16,1024]{3,2,1,0:T(8,128)(2,1)}, u32[]{:S(2)}, u32[]{:S(2)}) collective-permute-start(bf16[2,4,16,1024]{3,2,1,0:T(8,128)(2,1)} %bitcast.14), channel_id=1, source_target_pairs={{0,448},{1,449},{2,450},{3,451},{4,452},{5,453},{6,454},{7,455},{8... | collective-permute-start | bytes 786440 | tf_op jit(solution)/shard_map/ppermute | solution.py:59
  112.5 24.5 %copy-start.3 = (s32[64]{0:T(128)S(1)}, s32[64]{0:T(128)}, u32[]{:S(2)}) copy-start(s32[64]{0:T(128)} %points.1) | copy-start | bytes 772

commit v2 on v1

--- a/solution.py
+++ b/solution.py
@@ -34,6 +34,15 @@
 def along_z(step):
     def move(place):
         z = (place["zh"] * 4 + place["zl"] + step) % 16
+        place["zh"], place["zl"] = z // 4, z % 4
+
+    return routes(move)
+
+
+def along_z_by_core(step):
+    def move(place):
+        way = step if place["c"] else -step
+        z = (place["zh"] * 4 + place["zl"] + way) % 16
         place["zh"], place["zl"] = z // 4, z % 4
 
     return routes(move)
@@ -100,26 +109,24 @@
     return copies
 
 
-def own_kernel(where, m0, m1, mf, mh, mg, here, up, down, lower, upper, dens, na, nf, nh, out, xs, kept, *scratch):
+def own_kernel(where, ma, mf, mh, mg, here, up, two, down, dens, na, nf, nh, out, xs, kept, *scratch):
     sets, stage, sems = scratch
     yl, xl = where[3], where[4]
     copies = []
-    for piece, at, size in ((na, 0, 2), (nf, 2, 3), (nh, 5, 2)):
-        copies.append(pltpu.make_async_copy(piece, xs.at[pl.ds(at, size)], sems.at[2 + at]))
+    for piece, target, at in ((na, xs.at[:2], 2), (nf, xs.at[2:6], 4), (nh, xs.at[6], 5)):
+        copies.append(pltpu.make_async_copy(piece, target, sems.at[at]))
         copies[-1].start()
-    planes = ((here,), (up,), (lower, upper), (down,))
+    planes = (here, up, two, down)
     for dxl in range(2):
         for dyl in range(2):
             run = jnp.bitwise_xor(yl, dyl) * 2 + jnp.bitwise_xor(xl, dxl)
             at = 0
-            for blocks in planes:
-                for block in blocks:
-                    size = block.shape[0] * 16
-                    sets[dxl * 2 + dyl, at : at + size] = block[:, run].reshape(size, 1024)
-                    at += size
+            for block in planes:
+                sets[dxl * 2 + dyl, at : at + 64] = block[:, run].reshape(64, 1024)
+                at += 64
     copies.append(pltpu.make_async_copy(sets, kept, sems.at[3]))
     copies[-1].start()
-    groups = ((m0, mf.at[0], m1, mh.at[0]), (mf.at[1], mf.at[2], mg, mh.at[1]))
+    groups = ((ma.at[0], mf.at[0], ma.at[1], mf.at[3]), (mf.at[1], mf.at[2], mg, mh))
     copies += slab_products(where, 0, groups, sets, dens, stage, out, sems)
     for copy in copies:
         copy.wait()
@@ -191,18 +198,15 @@
     f3 = sent(orbitals, flip_y(3))
     g1 = sent(side, flip_y(1))
     g3 = sent(side, flip_y(3))
-    mg = sent(side, flip_y(2))
     ma = jnp.stack([orbitals, side])
     na = sent(ma, routes(flip_core))
     up = sent(here, along_z(-1))
     down = sent(here, along_z(1))
-    cuts = here[:2], here[2:]
-    lower = sent(cuts[0], along_z(-2))
-    upper = sent(cuts[1], along_z(2))
-    mf = jnp.stack([f1, f2, f3])
+    two = sent(here, along_z_by_core(2))
+    mg = sent(f2, routes(flip_x))
+    mf = jnp.stack([f1, f2, f3, g1])
     nf = sent(mf, routes(flip_core))
-    mh = jnp.stack([g1, g3])
-    nh = sent(mh, routes(flip_core))
+    nh = sent(g3, routes(flip_core))
     ng = sent(mg, routes(flip_core))
 
     orb = lax.axis_index(ORB)
@@ -220,7 +224,7 @@
             jax.ShapeDtypeStruct((7, rows, width), orbitals.dtype),
             jax.ShapeDtypeStruct((4, 256, width), orbitals.dtype),
         ),
-        in_specs=[smem] + [vmem] * 11 + [anywhere] * 3,
+        in_specs=[smem] + [vmem] * 9 + [anywhere] * 3,
         out_specs=(anywhere,) * 3,
         scratch_shapes=[
             pltpu.VMEM((4, 256, width), orbitals.dtype),
@@ -229,7 +233,7 @@
         ],
         compiler_params=PARAMS,
         name="own_products",
-    )(where, orbitals, side, mf, mh, mg, here, up, down, lower, upper, dens, na, nf, nh)
+    )(where, ma, mf, g3, mg, here, up, two, down, dens, na, nf, nh)
     blocks = pl.pallas_call(
         other_kernel,
         out_shape=shape,

time: 140 us -> 147 us (1.050)
  waiting for transfers between devices: 22.1 us -> 33.7 us
  local copies, waits for them, and re-layouts: 3.81 us -> 1.9 us
  blocking collectives: 24.5 us -> 22.9 us
    ppermute x15 -> x14, waiting for transfers between devices: 22.1 us -> 33.7 us  [sent(): return lax.ppermute(value, AXES, pairs)]
    all_to_all x1, blocking collectives: 24.5 us -> 22.9 us  [program(): lax.all_to_all(blocks.reshape(32, 72, 128), PLANE, split_axis=0, concat_a...]
    ppermute x15 -> x14, starting transfers between devices: 56.5 us -> 55.5 us  [sent(): return lax.ppermute(value, AXES, pairs)]
  transfers between devices with their start and end apart: 16 -> 15, of which waited for: 4 -> 5; matrix products, arithmetic and copies ran while one was open for 4% -> 3% of each run, Pallas kernels for 4% -> 4%
where the time goes in v2:
time: 147 us; the launch traced here: 146 us
  starting transfers between devices  71.4 us (49%)
  waiting for transfers between devices  33.7 us (23%)
  blocking collectives  22.9 us (16%)
  Pallas kernels  11.3 us (8%)
  other arithmetic  4.04 us (3%)
  local copies, waits for them, and re-layouts  1.9 us (1%)
    ppermute x14, starting transfers between devices, sent(): return lax.ppermute(value, AXES, pairs)  55.5 us
    ppermute x14, waiting for transfers between devices, sent(): return lax.ppermute(value, AXES, pairs)  33.7 us
    all_to_all x1, blocking collectives, program(): lax.all_to_all(blocks.reshape(32, 72, 128), PLANE, split_axis=0, concat_a...  22.9 us
    all_to_all x1, starting transfers between devices, program(): lax.all_to_all(quarters.reshape(16, 16, width), ('zh', 'yl', 'xl'), split...  15.9 us
    pallas_call x1, Pallas kernels, program(): pl.pallas_call(own_kernel, out_shape=(shape, jax.ShapeDtypeStruct((7, row...  4.87 us
    pallas_call x1, Pallas kernels, program(): pl.pallas_call(other_kernel, out_shape=shape, in_specs=[smem] + [vmem] *...  3.71 us
  transfers between devices with their start and end apart: 15, of which 5 were waited for; matrix products, arithmetic and copies ran while one was open for 3% of the time, Pallas kernels for 4%

profile of v2, /device:TPU:1, one launch (start us, length us, event | category | flops | bytes accessed | tf_op | source)
XLA Modules:
  0.0 146.1 jit_solution(9929468384401226272)
XLA Ops:
  0.6 3.9 %collective-permute-start = (bf16[256,1024]{1,0:T(8,128)(2,1)}, bf16[256,1024]{1,0:T(8,128)(2,1)S(1)}, u32[]{:S(2)}, u32[]{:S(2)}) collective-permute-start(bf16[256,1024]{1,0:T(8,128)(2,1)} %orbitals.1), channel_id=1, source_target_pairs={{0,1},{1,0},{2,3},{3,2},{4,5},{5,4},{6,7},{7,6},{8,9},{9,8},{10,11... | collective-permute-start | bytes 1572872 | tf_op jit(solution)/shard_map/ppermute | solution.py:68
  4.6 4.8 %collective-permute-start.2 = (bf16[256,1024]{1,0:T(8,128)(2,1)}, bf16[256,1024]{1,0:T(8,128)(2,1)}, u32[]{:S(2)}, u32[]{:S(2)}) collective-permute-start(bf16[256,1024]{1,0:T(8,128)(2,1)} %orbitals.1), channel_id=1, source_target_pairs={{0,16},{1,17},{2,18},{3,19},{4,20},{5,21},{6,22},{7,23},{8,24},{9,... | collective-permute-start | bytes 1572872 | tf_op jit(solution)/shard_map/ppermute | solution.py:68
  9.4 2.7 %collective-permute-start.3 = (bf16[256,1024]{1,0:T(8,128)(2,1)}, bf16[256,1024]{1,0:T(8,128)(2,1)S(1)}, u32[]{:S(2)}, u32[]{:S(2)}) collective-permute-start(bf16[256,1024]{1,0:T(8,128)(2,1)} %orbitals.1), channel_id=1, source_target_pairs={{0,20},{1,21},{2,22},{3,23},{4,16},{5,17},{6,18},{7,19},{8,28},{9,... | collective-permute-start | bytes 1572872 | tf_op jit(solution)/shard_map/ppermute | solution.py:68
  12.1 1.9 %collective-permute-start.1 = (bf16[256,1024]{1,0:T(8,128)(2,1)}, bf16[256,1024]{1,0:T(8,128)(2,1)S(1)}, u32[]{:S(2)}, u32[]{:S(2)}) collective-permute-start(bf16[256,1024]{1,0:T(8,128)(2,1)} %orbitals.1), channel_id=1, source_target_pairs={{0,4},{1,5},{2,6},{3,7},{4,0},{5,1},{6,2},{7,3},{8,12},{9,13},{10,... | collective-permute-start | bytes 1572872 | tf_op jit(solution)/shard_map/ppermute | solution.py:68
  14.1 5.6 %collective-permute-start.4 = (bf16[256,1024]{1,0:T(8,128)(2,1)S(1)}, bf16[256,1024]{1,0:T(8,128)(2,1)}, u32[]{:S(2)}, u32[]{:S(2)}) collective-permute-start(bf16[256,1024]{1,0:T(8,128)(2,1)S(1)} %collective-permute-done), channel_id=1, source_target_pairs={{0,4},{1,5},{2,6},{3,7},{4,0},{5,1},{6,2},{7,3},{8,12},{9,13},{10,... | collective-permute-start | bytes 1572872 | tf_op jit(solution)/shard_map/ppermute | solution.py:68
  22.4 15.9 %all-to-all-start = ((bf16[16,16,1024]{2,1,0:T(8,128)(2,1)}), bf16[16,16,1024]{2,1,0:T(8,128)(2,1)}, u32[]{:S(2)}, u32[]{:S(2)}) async-start(bf16[16,16,1024]{2,1,0:T(8,128)(2,1)} %bitcast.13), calls=%async_computation | async-start | bytes 1048576 | tf_op jit(solution)/shard_map/all_to_all | solution.py:188
  38.4 5.7 %collective-permute-done.4 = bf16[256,1024]{1,0:T(8,128)(2,1)} collective-permute-done((bf16[256,1024]{1,0:T(8,128)(2,1)S(1)}, bf16[256,1024]{1,0:T(8,128)(2,1)}, u32[]{:S(2)}, u32[]{:S(2)}) %collective-permute-start.4) | collective-permute-done | bytes 524320 | tf_op jit(solution)/shard_map/ppermute | solution.py:68
  44.0 1.8 %pad_maximum_fusion.mf = bf16[4,256,1024]{2,1,0:T(8,128)(2,1)S(1)} fusion(bf16[1,256,1024]{2,1,0:T(8,128)(2,1)} %bitcast.11, bf16[1,256,1024]{2,1,0:T(8,128)(2,1)} %bitcast.22, bf16[1,256,1024]{2,1,0:T(8,128)(2,1)} %bitcast.9, bf16[1,256,1024]{2,1,0:T(8,128)(2,1)} %bitcast.23), kind=kLoop, calls=%fused_computation | loop fusion | flops 3145728 | bytes 4194304 | tf_op jit(solution)/shard_map/stack | solution.py:207
  45.9 4.4 %collective-permute-start.11 = (bf16[4,256,1024]{2,1,0:T(8,128)(2,1)S(1)}, bf16[4,256,1024]{2,1,0:T(8,128)(2,1)}, u32[]{:S(2)}, u32[]{:S(2)}) collective-permute-start(bf16[4,256,1024]{2,1,0:T(8,128)(2,1)S(1)} %pad_maximum_fusion.mf), channel_id=1, source_target_pairs={{0,8},{1,9},{2,10},{3,11},{4,12},{5,13},{6,14},{7,15},{8,0},{9,1},... | collective-permute-start | bytes 6291464 | tf_op jit(solution)/shard_map/ppermute | solution.py:68
  51.5 1.9 %collective-permute-start.10 = (bf16[2,256,1024]{2,1,0:T(8,128)(2,1)S(1)}, bf16[2,256,1024]{2,1,0:T(8,128)(2,1)}, u32[]{:S(2)}, u32[]{:S(2)}) collective-permute-start(bf16[2,256,1024]{2,1,0:T(8,128)(2,1)S(1)} %pad_maximum_fusion.1.ma), channel_id=1, source_target_pairs={{0,8},{1,9},{2,10},{3,11},{4,12},{5,13},{6,14},{7,15},{8,0},{9,1},... | collective-permute-start | bytes 3145736 | tf_op jit(solution)/shard_map/ppermute | solution.py:68
  53.5 1.9 %collective-permute-start.5 = (bf16[256,1024]{1,0:T(8,128)(2,1)S(1)}, bf16[256,1024]{1,0:T(8,128)(2,1)}, u32[]{:S(2)}, u32[]{:S(2)}) collective-permute-start(bf16[256,1024]{1,0:T(8,128)(2,1)S(1)} %copy-done.5), channel_id=1, source_target_pairs={{0,20},{1,21},{2,22},{3,23},{4,16},{5,17},{6,18},{7,19},{8,28},{9,... | collective-permute-start | bytes 1572872 | tf_op jit(solution)/shard_map/ppermute | solution.py:68
  55.4 3.2 %collective-permute-start.6 = (bf16[256,1024]{1,0:T(8,128)(2,1)}, bf16[256,1024]{1,0:T(8,128)(2,1)}, u32[]{:S(2)}, u32[]{:S(2)}) collective-permute-start(bf16[256,1024]{1,0:T(8,128)(2,1)} %collective-permute-done.2), channel_id=1, source_target_pairs={{0,1},{1,0},{2,3},{3,2},{4,5},{5,4},{6,7},{7,6},{8,9},{9,8},{10,11... | collective-permute-start | bytes 1572872 | tf_op jit(solution)/shard_map/ppermute | solution.py:68
  58.6 11.1 %collective-permute-done.5.mh = bf16[256,1024]{1,0:T(8,128)(2,1)} collective-permute-done((bf16[256,1024]{1,0:T(8,128)(2,1)S(1)}, bf16[256,1024]{1,0:T(8,128)(2,1)}, u32[]{:S(2)}, u32[]{:S(2)}) %collective-permute-start.5) | collective-permute-done | bytes 524320 | tf_op jit(solution)/shard_map/ppermute | solution.py:68
  69.7 3.3 %collective-permute-start.12 = (bf16[256,1024]{1,0:T(8,128)(2,1)}, bf16[256,1024]{1,0:T(8,128)(2,1)}, u32[]{:S(2)}, u32[]{:S(2)}) collective-permute-start(bf16[256,1024]{1,0:T(8,128)(2,1)} %collective-permute-done.5.mh), channel_id=1, source_target_pairs={{0,8},{1,9},{2,10},{3,11},{4,12},{5,13},{6,14},{7,15},{8,0},{9,1},... | collective-permute-start | bytes 1572872 | tf_op jit(solution)/shard_map/ppermute | solution.py:68
  73.0 14.3 %collective-permute-start.7 = (bf16[4,4,16,1024]{3,2,1,0:T(8,128)(2,1)}, bf16[4,4,16,1024]{3,2,1,0:T(8,128)(2,1)}, u32[]{:S(2)}, u32[]{:S(2)}) collective-permute-start(bf16[4,4,16,1024]{3,2,1,0:T(8,128)(2,1)} %bitcast.14.here), channel_id=1, source_target_pairs={{0,480},{1,481},{2,482},{3,483},{4,484},{5,485},{6,486},{7,487},{8... | collective-permute-start | bytes 1572872 | tf_op jit(solution)/shard_map/ppermute | solution.py:68
  87.2 1.9 %collective-permute-start.8 = (bf16[4,4,16,1024]{3,2,1,0:T(8,128)(2,1)}, bf16[4,4,16,1024]{3,2,1,0:T(8,128)(2,1)}, u32[]{:S(2)}, u32[]{:S(2)}) collective-permute-start(bf16[4,4,16,1024]{3,2,1,0:T(8,128)(2,1)} %bitcast.14.here), channel_id=1, source_target_pairs={{0,448},{1,449},{2,450},{3,451},{4,452},{5,453},{6,454},{7,455},{8... | collective-permute-start | bytes 1572872 | tf_op jit(solution)/shard_map/ppermute | solution.py:68
  89.2 1.9 %collective-permute-start.9 = (bf16[4,4,16,1024]{3,2,1,0:T(8,128)(2,1)}, bf16[4,4,16,1024]{3,2,1,0:T(8,128)(2,1)}, u32[]{:S(2)}, u32[]{:S(2)}) collective-permute-start(bf16[4,4,16,1024]{3,2,1,0:T(8,128)(2,1)} %bitcast.14.here), channel_id=1, source_target_pairs={{0,32},{1,33},{2,34},{3,35},{4,36},{5,37},{6,38},{7,39},{8,40},{9,... | collective-permute-start | bytes 1572872 | tf_op jit(solution)/shard_map/ppermute | solution.py:68
  91.1 3.7 %collective-permute-start.13 = (bf16[256,1024]{1,0:T(8,128)(2,1)}, bf16[256,1024]{1,0:T(8,128)(2,1)}, u32[]{:S(2)}, u32[]{:S(2)}) collective-permute-start(bf16[256,1024]{1,0:T(8,128)(2,1)} %collective-permute-done.6.mg), channel_id=1, source_target_pairs={{0,8},{1,9},{2,10},{3,11},{4,12},{5,13},{6,14},{7,15},{8,0},{9,1},... | collective-permute-start | bytes 1572872 | tf_op jit(solution)/shard_map/ppermute | solution.py:68
  96.0 8.4 %collective-permute-done.7.up = bf16[4,4,16,1024]{3,2,1,0:T(8,128)(2,1)} collective-permute-done((bf16[4,4,16,1024]{3,2,1,0:T(8,128)(2,1)}, bf16[4,4,16,1024]{3,2,1,0:T(8,128)(2,1)}, u32[]{:S(2)}, u32[]{:S(2)}) %collective-permute-start.7) | collective-permute-done | bytes 524320 | tf_op jit(solution)/shard_map/ppermute | solution.py:68
  104.4 4.2 %collective-permute-done.8.two = bf16[4,4,16,1024]{3,2,1,0:T(8,128)(2,1)} collective-permute-done((bf16[4,4,16,1024]{3,2,1,0:T(8,128)(2,1)}, bf16[4,4,16,1024]{3,2,1,0:T(8,128)(2,1)}, u32[]{:S(2)}, u32[]{:S(2)}) %collective-permute-start.8) | collective-permute-done | bytes 524320 | tf_op jit(solution)/shard_map/ppermute | solution.py:68
  108.6 4.3 %collective-permute-done.9.down = bf16[4,4,16,1024]{3,2,1,0:T(8,128)(2,1)} collective-permute-done((bf16[4,4,16,1024]{3,2,1,0:T(8,128)(2,1)}, bf16[4,4,16,1024]{3,2,1,0:T(8,128)(2,1)}, u32[]{:S(2)}, u32[]{:S(2)}) %collective-permute-start.9) | collective-permute-done | bytes 524320 | tf_op jit(solution)/shard_map/ppermute | solution.py:68
  112.9 4.9 %own_products.1 = (f32[4,8,72,128]{3,2,1,0:T(8,128)S(1)}, bf16[7,256,1024]{2,1,0:T(8,128)(2,1)S(1)}, bf16[4,256,1024]{2,1,0:T(8,128)(2,1)S(1)}) custom-call(s32[6]{0:T(128)S(1)} %stack.51.where, bf16[2,256,1024]{2,1,0:T(8,128)(2,1)S(1)} %pad_maximum_fusion.1.ma, bf16[4,256,1024]{2,1,0:T(8,128)(2,1)S(1)} %pad_maximum_fusion.mf, ...), custom_call_target="tpu_custom_call" | custom-call | tf_op jit(solution)/shard_map/own_products/pallas_call | solution.py:220
  117.8 3.7 %other_products.1 = f32[4,8,72,128]{3,2,1,0:T(8,128)S(1)} custom-call(s32[6]{0:T(128)S(1)} %stack.51.where, bf16[7,256,1024]{2,1,0:T(8,128)(2,1)S(1)} %get-tuple-element.6.xs, bf16[256,1024]{1,0:T(8,128)(2,1)} %collective-permute-done.13.ng, bf16[4,256,1024]{2,1,0:T(8,128)(2,1)S(1)} %get-tuple-element.7.kept, ...), custom_call_target="tpu_custom_call", output_to_operand_aliasing={{}: (5, {})} | custom-call | tf_op jit(solution)/shard_map/other_products/pallas_call | solution.py:237
  121.6 22.9 %all_to_all.10 = f32[32,72,128]{2,1,0:T(8,128)S(1)} all-to-all(f32[32,72,128]{2,1,0:T(8,128)S(1)} %bitcast.18), channel_id=1, replica_groups=mesh['zh'=4,'zl'=4,'yh'=2,'c'=2,'yl'=2,'xh'=2,'xl'=2] {'yh','c','yl','xh..., dimensions={0} | all-to-all | bytes 2359296 | tf_op jit(solution)/shard_map/all_to_all | solution.py:250
  (34 shorter events, 6.8 us)
Async XLA Ops:
  0.6 13.4 %collective-permute-start = (bf16[256,1024]{1,0:T(8,128)(2,1)}, bf16[256,1024]{1,0:T(8,128)(2,1)S(1)}, u32[]{:S(2)}, u32[]{:S(2)}) collective-permute-start(bf16[256,1024]{1,0:T(8,128)(2,1)} %orbitals.1), channel_id=1, source_target_pairs={{0,1},{1,0},{2,3},{3,2},{4,5},{5,4},{6,7},{7,6},{8,9},{9,8},{10,11... | collective-permute-start | bytes 1572872 | tf_op jit(solution)/shard_map/ppermute | solution.py:68
  4.6 33.7 %collective-permute-start.2 = (bf16[256,1024]{1,0:T(8,128)(2,1)}, bf16[256,1024]{1,0:T(8,128)(2,1)}, u32[]{:S(2)}, u32[]{:S(2)}) collective-permute-start(bf16[256,1024]{1,0:T(8,128)(2,1)} %orbitals.1), channel_id=1, source_target_pairs={{0,16},{1,17},{2,18},{3,19},{4,20},{5,21},{6,22},{7,23},{8,24},{9,... | collective-permute-start | bytes 1572872 | tf_op jit(solution)/shard_map/ppermute | solution.py:68
  9.4 28.9 %collective-permute-start.3 = (bf16[256,1024]{1,0:T(8,128)(2,1)}, bf16[256,1024]{1,0:T(8,128)(2,1)S(1)}, u32[]{:S(2)}, u32[]{:S(2)}) collective-permute-start(bf16[256,1024]{1,0:T(8,128)(2,1)} %orbitals.1), channel_id=1, source_target_pairs={{0,20},{1,21},{2,22},{3,23},{4,16},{5,17},{6,18},{7,19},{8,28},{9,... | collective-permute-start | bytes 1572872 | tf_op jit(solution)/shard_map/ppermute | solution.py:68
  12.1 26.3 %collective-permute-start.1 = (bf16[256,1024]{1,0:T(8,128)(2,1)}, bf16[256,1024]{1,0:T(8,128)(2,1)S(1)}, u32[]{:S(2)}, u32[]{:S(2)}) collective-permute-start(bf16[256,1024]{1,0:T(8,128)(2,1)} %orbitals.1), channel_id=1, source_target_pairs={{0,4},{1,5},{2,6},{3,7},{4,0},{5,1},{6,2},{7,3},{8,12},{9,13},{10,... | collective-permute-start | bytes 1572872 | tf_op jit(solution)/shard_map/ppermute | solution.py:68
  14.0 31.8 %copy-start.4 = (bf16[256,1024]{1,0:T(8,128)(2,1)}, bf16[256,1024]{1,0:T(8,128)(2,1)S(1)}, u32[]{:S(2)}) copy-start(bf16[256,1024]{1,0:T(8,128)(2,1)S(1)} %collective-permute-done) | copy-start | bytes 1572868
  14.1 30.0 %collective-permute-start.4 = (bf16[256,1024]{1,0:T(8,128)(2,1)S(1)}, bf16[256,1024]{1,0:T(8,128)(2,1)}, u32[]{:S(2)}, u32[]{:S(2)}) collective-permute-start(bf16[256,1024]{1,0:T(8,128)(2,1)S(1)} %collective-permute-done), channel_id=1, source_target_pairs={{0,4},{1,5},{2,6},{3,7},{4,0},{5,1},{6,2},{7,3},{8,12},{9,13},{10,... | collective-permute-start | bytes 1572872 | tf_op jit(solution)/shard_map/ppermute | solution.py:68
  19.7 1.0 copy-start
  20.7 0.7 copy-start.2
  22.4 50.5 %all-to-all-start = ((bf16[16,16,1024]{2,1,0:T(8,128)(2,1)}), bf16[16,16,1024]{2,1,0:T(8,128)(2,1)}, u32[]{:S(2)}, u32[]{:S(2)}) async-start(bf16[16,16,1024]{2,1,0:T(8,128)(2,1)} %bitcast.13), calls=%async_computation | async-start | bytes 1048576 | tf_op jit(solution)/shard_map/all_to_all | solution.py:188
  38.3 5.7 %copy-start.6 = (bf16[256,1024]{1,0:T(8,128)(2,1)}, bf16[256,1024]{1,0:T(8,128)(2,1)S(1)}, u32[]{:S(2)}) copy-start(bf16[256,1024]{1,0:T(8,128)(2,1)S(1)} %collective-permute-done.3) | copy-start | bytes 1572868
  38.4 5.7 %copy-start.7 = (bf16[256,1024]{1,0:T(8,128)(2,1)}, bf16[256,1024]{1,0:T(8,128)(2,1)S(1)}, u32[]{:S(2)}) copy-start(bf16[256,1024]{1,0:T(8,128)(2,1)S(1)} %collective-permute-done.1) | copy-start | bytes 1572868
  44.0 6.3 %copy-start.1 = (bf16[256,1024]{1,0:T(8,128)(2,1)S(1)}, bf16[256,1024]{1,0:T(8,128)(2,1)}, u32[]{:S(2)}) copy-start(bf16[256,1024]{1,0:T(8,128)(2,1)} %orbitals.1) | copy-start | bytes 1572868
  45.9 67.1 %collective-permute-start.11 = (bf16[4,256,1024]{2,1,0:T(8,128)(2,1)S(1)}, bf16[4,256,1024]{2,1,0:T(8,128)(2,1)}, u32[]{:S(2)}, u32[]{:S(2)}) collective-permute-start(bf16[4,256,1024]{2,1,0:T(8,128)(2,1)S(1)} %pad_maximum_fusion.mf), channel_id=1, source_target_pairs={{0,8},{1,9},{2,10},{3,11},{4,12},{5,13},{6,14},{7,15},{8,0},{9,1},... | collective-permute-start | bytes 6291464 | tf_op jit(solution)/shard_map/ppermute | solution.py:68
  50.3 3.2 %copy-start.5 = (bf16[256,1024]{1,0:T(8,128)(2,1)S(1)}, bf16[256,1024]{1,0:T(8,128)(2,1)}, u32[]{:S(2)}) copy-start(bf16[256,1024]{1,0:T(8,128)(2,1)} %copy-done.4) | copy-start | bytes 1572868
  51.5 37.6 %collective-permute-start.10 = (bf16[2,256,1024]{2,1,0:T(8,128)(2,1)S(1)}, bf16[2,256,1024]{2,1,0:T(8,128)(2,1)}, u32[]{:S(2)}, u32[]{:S(2)}) collective-permute-start(bf16[2,256,1024]{2,1,0:T(8,128)(2,1)S(1)} %pad_maximum_fusion.1.ma), channel_id=1, source_target_pairs={{0,8},{1,9},{2,10},{3,11},{4,12},{5,13},{6,14},{7,15},{8,0},{9,1},... | collective-permute-start | bytes 3145736 | tf_op jit(solution)/shard_map/ppermute | solution.py:68
  53.5 16.2 %collective-permute-start.5 = (bf16[256,1024]{1,0:T(8,128)(2,1)S(1)}, bf16[256,1024]{1,0:T(8,128)(2,1)}, u32[]{:S(2)}, u32[]{:S(2)}) collective-permute-start(bf16[256,1024]{1,0:T(8,128)(2,1)S(1)} %copy-done.5), channel_id=1, source_target_pairs={{0,20},{1,21},{2,22},{3,23},{4,16},{5,17},{6,18},{7,19},{8,28},{9,... | collective-permute-start | bytes 1572872 | tf_op jit(solution)/shard_map/ppermute | solution.py:68
  55.4 31.8 %collective-permute-start.6 = (bf16[256,1024]{1,0:T(8,128)(2,1)}, bf16[256,1024]{1,0:T(8,128)(2,1)}, u32[]{:S(2)}, u32[]{:S(2)}) collective-permute-start(bf16[256,1024]{1,0:T(8,128)(2,1)} %collective-permute-done.2), channel_id=1, source_target_pairs={{0,1},{1,0},{2,3},{3,2},{4,5},{5,4},{6,7},{7,6},{8,9},{9,8},{10,11... | collective-permute-start | bytes 1572872 | tf_op jit(solution)/shard_map/ppermute | solution.py:68
  69.7 21.4 %collective-permute-start.12 = (bf16[256,1024]{1,0:T(8,128)(2,1)}, bf16[256,1024]{1,0:T(8,128)(2,1)}, u32[]{:S(2)}, u32[]{:S(2)}) collective-permute-start(bf16[256,1024]{1,0:T(8,128)(2,1)} %collective-permute-done.5.mh), channel_id=1, source_target_pairs={{0,8},{1,9},{2,10},{3,11},{4,12},{5,13},{6,14},{7,15},{8,0},{9,1},... | collective-permute-start | bytes 1572872 | tf_op jit(solution)/shard_map/ppermute | solution.py:68
  73.0 31.5 %collective-permute-start.7 = (bf16[4,4,16,1024]{3,2,1,0:T(8,128)(2,1)}, bf16[4,4,16,1024]{3,2,1,0:T(8,128)(2,1)}, u32[]{:S(2)}, u32[]{:S(2)}) collective-permute-start(bf16[4,4,16,1024]{3,2,1,0:T(8,128)(2,1)} %bitcast.14.here), channel_id=1, source_target_pairs={{0,480},{1,481},{2,482},{3,483},{4,484},{5,485},{6,486},{7,487},{8... | collective-permute-start | bytes 1572872 | tf_op jit(solution)/shard_map/ppermute | solution.py:68
  87.2 21.4 %collective-permute-start.8 = (bf16[4,4,16,1024]{3,2,1,0:T(8,128)(2,1)}, bf16[4,4,16,1024]{3,2,1,0:T(8,128)(2,1)}, u32[]{:S(2)}, u32[]{:S(2)}) collective-permute-start(bf16[4,4,16,1024]{3,2,1,0:T(8,128)(2,1)} %bitcast.14.here), channel_id=1, source_target_pairs={{0,448},{1,449},{2,450},{3,451},{4,452},{5,453},{6,454},{7,455},{8... | collective-permute-start | bytes 1572872 | tf_op jit(solution)/shard_map/ppermute | solution.py:68
  89.2 23.8 %collective-permute-start.9 = (bf16[4,4,16,1024]{3,2,1,0:T(8,128)(2,1)}, bf16[4,4,16,1024]{3,2,1,0:T(8,128)(2,1)}, u32[]{:S(2)}, u32[]{:S(2)}) collective-permute-start(bf16[4,4,16,1024]{3,2,1,0:T(8,128)(2,1)} %bitcast.14.here), channel_id=1, source_target_pairs={{0,32},{1,33},{2,34},{3,35},{4,36},{5,37},{6,38},{7,39},{8,40},{9,... | collective-permute-start | bytes 1572872 | tf_op jit(solution)/shard_map/ppermute | solution.py:68
  91.1 26.7 %collective-permute-start.13 = (bf16[256,1024]{1,0:T(8,128)(2,1)}, bf16[256,1024]{1,0:T(8,128)(2,1)}, u32[]{:S(2)}, u32[]{:S(2)}) collective-permute-start(bf16[256,1024]{1,0:T(8,128)(2,1)} %collective-permute-done.6.mg), channel_id=1, source_target_pairs={{0,8},{1,9},{2,10},{3,11},{4,12},{5,13},{6,14},{7,15},{8,0},{9,1},... | collective-permute-start | bytes 1572872 | tf_op jit(solution)/shard_map/ppermute | solution.py:68
  121.6 22.9 %copy-start.3 = (s32[64]{0:T(128)S(1)}, s32[64]{0:T(128)}, u32[]{:S(2)}) copy-start(s32[64]{0:T(128)} %points.1) | copy-start | bytes 772

commit v3 on v2

--- a/solution.py
+++ b/solution.py
@@ -103,13 +103,13 @@
                 stage[dyh, orb, pl.ds(base_row, 16), :] = part[:, :128]
                 stage[dyh, orb, pl.ds(base_row + 16, 16), :] = part[:, 128:]
         for orb in range(8):
-            stage[dyh, orb, 64:72, :] = dens[...]
+            stage[dyh, orb, 64:72, :] = dens if dyh == 0 else jnp.zeros_like(dens)
         copies.append(pltpu.make_async_copy(stage.at[dyh], out.at[slab], sems.at[dyh]))
         copies[-1].start()
     return copies
 
 
-def own_kernel(where, ma, mf, mh, mg, here, up, two, down, dens, na, nf, nh, out, xs, kept, *scratch):
+def own_kernel(where, ma, mf, mh, mg, here, up, two, down, quarters, na, nf, nh, out, xs, kept, *scratch):
     sets, stage, sems = scratch
     yl, xl = where[3], where[4]
     copies = []
@@ -127,17 +127,26 @@
     copies.append(pltpu.make_async_copy(sets, kept, sems.at[3]))
     copies[-1].start()
     groups = ((ma.at[0], mf.at[0], ma.at[1], mf.at[3]), (mf.at[1], mf.at[2], mg, mh))
+    chosen = quarters[0].reshape(64, 1024).astype(jnp.float32)
+    dens = lax.dot_general(
+        jnp.ones((8, 1024), jnp.float32),
+        chosen * chosen,
+        (((1,), (1,)), ((), ())),
+        precision=lax.Precision.HIGHEST,
+        preferred_element_type=jnp.float32,
+    )
+    dens = jnp.concatenate([dens, jnp.zeros_like(dens)], axis=1)
     copies += slab_products(where, 0, groups, sets, dens, stage, out, sems)
     for copy in copies:
         copy.wait()
 
 
-def other_kernel(where, xs, ng, kept, dens, _, out, stage, sems):
+def other_kernel(where, xs, ng, kept, _, out, stage, sems):
     groups = (
         (xs.at[0], xs.at[2], xs.at[1], xs.at[5]),
         (xs.at[3], xs.at[4], ng, xs.at[6]),
     )
-    for copy in slab_products(where, 1, groups, kept, dens, stage, out, sems):
+    for copy in slab_products(where, 1, groups, kept, jnp.zeros((8, 128), jnp.float32), stage, out, sems):
         copy.wait()
 
 
@@ -181,10 +190,6 @@
         compiler_params=PARAMS,
         name="pick",
     )(points.reshape(1, mu_dev), orbitals)
-    chosen_wide = quarters[0].reshape(mu_dev, width).astype(jnp.float32)
-    dens = jnp.sum(chosen_wide * chosen_wide, axis=1)
-    dens = jnp.broadcast_to(jnp.concatenate([dens, jnp.zeros_like(dens)])[None], (8, 128))
-
     here = lax.all_to_all(
         quarters.reshape(16, 16, width),
         ("zh", "yl", "xl"),
@@ -233,20 +238,20 @@
         ],
         compiler_params=PARAMS,
         name="own_products",
-    )(where, ma, mf, g3, mg, here, up, two, down, dens, na, nf, nh)
+    )(where, ma, mf, g3, mg, here, up, two, down, quarters, na, nf, nh)
     blocks = pl.pallas_call(
         other_kernel,
         out_shape=shape,
-        in_specs=[smem] + [vmem] * 4 + [anywhere],
+        in_specs=[smem] + [vmem] * 3 + [anywhere],
         out_specs=anywhere,
         scratch_shapes=[
             pltpu.VMEM((2, 8, 72, 128), jnp.float32),
             pltpu.SemaphoreType.DMA((2,)),
         ],
-        input_output_aliases={5: 0},
+        input_output_aliases={4: 0},
         compiler_params=PARAMS,
         name="other_products",
-    )(where, xs, ng, kept, dens, blocks)
+    )(where, xs, ng, kept, blocks)
     parts = lax.all_to_all(
         blocks.reshape(32, 72, 128), PLANE, split_axis=0, concat_axis=0, tiled=True
     ).reshape(2, 2, 2, 2, 2, 72, 128)

time: 147 us -> 147 us (level)
  transfers between devices with their start and end apart: 15 -> 15, of which waited for: 5 -> 5; matrix products, arithmetic and copies ran while one was open for 3% -> 2% of each run, Pallas kernels for 4% -> 4%
where the time goes in v3:
time: 147 us; the launch traced here: 146 us
  starting transfers between devices  71.4 us (49%)
  waiting for transfers between devices  34.8 us (24%)
  blocking collectives  22.9 us (16%)
  Pallas kernels  11.2 us (8%)
  other arithmetic  2.87 us (2%)
  local copies, waits for them, and re-layouts  1.8 us (1%)
    ppermute x14, starting transfers between devices, sent(): return lax.ppermute(value, AXES, pairs)  55.5 us
    ppermute x14, waiting for transfers between devices, sent(): return lax.ppermute(value, AXES, pairs)  34.8 us
    all_to_all x1, blocking collectives, program(): lax.all_to_all(blocks.reshape(32, 72, 128), PLANE, split_axis=0, concat_a...  22.9 us
    all_to_all x1, starting transfers between devices, program(): lax.all_to_all(quarters.reshape(16, 16, width), ('zh', 'yl', 'xl'), split...  15.9 us
    pallas_call x1, Pallas kernels, program(): pl.pallas_call(own_kernel, out_shape=(shape, jax.ShapeDtypeStruct((7, row...  4.82 us
    pallas_call x1, Pallas kernels, program(): pl.pallas_call(other_kernel, out_shape=shape, in_specs=[smem] + [vmem] *...  3.71 us
  transfers between devices with their start and end apart: 15, of which 5 were waited for; matrix products, arithmetic and copies ran while one was open for 2% of the time, Pallas kernels for 4%

profile of v3, /device:TPU:1, one launch (start us, length us, event | category | flops | bytes accessed | tf_op | source)
XLA Modules:
  0.0 145.9 jit_solution(14617713246673763492)
XLA Ops:
  0.6 3.9 %collective-permute-start = (bf16[256,1024]{1,0:T(8,128)(2,1)}, bf16[256,1024]{1,0:T(8,128)(2,1)S(1)}, u32[]{:S(2)}, u32[]{:S(2)}) collective-permute-start(bf16[256,1024]{1,0:T(8,128)(2,1)} %orbitals.1), channel_id=1, source_target_pairs={{0,1},{1,0},{2,3},{3,2},{4,5},{5,4},{6,7},{7,6},{8,9},{9,8},{10,11... | collective-permute-start | bytes 1572872 | tf_op jit(solution)/shard_map/ppermute | solution.py:68
  4.6 4.8 %collective-permute-start.2 = (bf16[256,1024]{1,0:T(8,128)(2,1)}, bf16[256,1024]{1,0:T(8,128)(2,1)}, u32[]{:S(2)}, u32[]{:S(2)}) collective-permute-start(bf16[256,1024]{1,0:T(8,128)(2,1)} %orbitals.1), channel_id=1, source_target_pairs={{0,16},{1,17},{2,18},{3,19},{4,20},{5,21},{6,22},{7,23},{8,24},{9,... | collective-permute-start | bytes 1572872 | tf_op jit(solution)/shard_map/ppermute | solution.py:68
  9.4 2.7 %collective-permute-start.3 = (bf16[256,1024]{1,0:T(8,128)(2,1)}, bf16[256,1024]{1,0:T(8,128)(2,1)S(1)}, u32[]{:S(2)}, u32[]{:S(2)}) collective-permute-start(bf16[256,1024]{1,0:T(8,128)(2,1)} %orbitals.1), channel_id=1, source_target_pairs={{0,20},{1,21},{2,22},{3,23},{4,16},{5,17},{6,18},{7,19},{8,28},{9,... | collective-permute-start | bytes 1572872 | tf_op jit(solution)/shard_map/ppermute | solution.py:68
  12.1 1.9 %collective-permute-start.1 = (bf16[256,1024]{1,0:T(8,128)(2,1)}, bf16[256,1024]{1,0:T(8,128)(2,1)S(1)}, u32[]{:S(2)}, u32[]{:S(2)}) collective-permute-start(bf16[256,1024]{1,0:T(8,128)(2,1)} %orbitals.1), channel_id=1, source_target_pairs={{0,4},{1,5},{2,6},{3,7},{4,0},{5,1},{6,2},{7,3},{8,12},{9,13},{10,... | collective-permute-start | bytes 1572872 | tf_op jit(solution)/shard_map/ppermute | solution.py:68
  14.1 5.6 %collective-permute-start.4 = (bf16[256,1024]{1,0:T(8,128)(2,1)S(1)}, bf16[256,1024]{1,0:T(8,128)(2,1)}, u32[]{:S(2)}, u32[]{:S(2)}) collective-permute-start(bf16[256,1024]{1,0:T(8,128)(2,1)S(1)} %collective-permute-done), channel_id=1, source_target_pairs={{0,4},{1,5},{2,6},{3,7},{4,0},{5,1},{6,2},{7,3},{8,12},{9,13},{10,... | collective-permute-start | bytes 1572872 | tf_op jit(solution)/shard_map/ppermute | solution.py:68
  22.4 15.9 %all-to-all-start = ((bf16[16,16,1024]{2,1,0:T(8,128)(2,1)}), bf16[16,16,1024]{2,1,0:T(8,128)(2,1)}, u32[]{:S(2)}, u32[]{:S(2)}) async-start(bf16[16,16,1024]{2,1,0:T(8,128)(2,1)} %bitcast.13), calls=%async_computation | async-start | bytes 1048576 | tf_op jit(solution)/shard_map/all_to_all | solution.py:193
  38.4 5.7 %collective-permute-done.4 = bf16[256,1024]{1,0:T(8,128)(2,1)} collective-permute-done((bf16[256,1024]{1,0:T(8,128)(2,1)S(1)}, bf16[256,1024]{1,0:T(8,128)(2,1)}, u32[]{:S(2)}, u32[]{:S(2)}) %collective-permute-start.4) | collective-permute-done | bytes 524320 | tf_op jit(solution)/shard_map/ppermute | solution.py:68
  44.0 1.7 %pad_maximum_fusion.mf = bf16[4,256,1024]{2,1,0:T(8,128)(2,1)S(1)} fusion(bf16[1,256,1024]{2,1,0:T(8,128)(2,1)} %bitcast.11, bf16[1,256,1024]{2,1,0:T(8,128)(2,1)S(1)} %bitcast.22, bf16[1,256,1024]{2,1,0:T(8,128)(2,1)} %bitcast.9, bf16[1,256,1024]{2,1,0:T(8,128)(2,1)} %bitcast.23), kind=kLoop, calls=%fused_computation | loop fusion | flops 3145728 | bytes 4194304 | tf_op jit(solution)/shard_map/stack | solution.py:212
  45.7 4.4 %collective-permute-start.11 = (bf16[4,256,1024]{2,1,0:T(8,128)(2,1)S(1)}, bf16[4,256,1024]{2,1,0:T(8,128)(2,1)}, u32[]{:S(2)}, u32[]{:S(2)}) collective-permute-start(bf16[4,256,1024]{2,1,0:T(8,128)(2,1)S(1)} %pad_maximum_fusion.mf), channel_id=1, source_target_pairs={{0,8},{1,9},{2,10},{3,11},{4,12},{5,13},{6,14},{7,15},{8,0},{9,1},... | collective-permute-start | bytes 6291464 | tf_op jit(solution)/shard_map/ppermute | solution.py:68
  51.4 1.9 %collective-permute-start.10 = (bf16[2,256,1024]{2,1,0:T(8,128)(2,1)S(1)}, bf16[2,256,1024]{2,1,0:T(8,128)(2,1)}, u32[]{:S(2)}, u32[]{:S(2)}) collective-permute-start(bf16[2,256,1024]{2,1,0:T(8,128)(2,1)S(1)} %pad_maximum_fusion.1.ma), channel_id=1, source_target_pairs={{0,8},{1,9},{2,10},{3,11},{4,12},{5,13},{6,14},{7,15},{8,0},{9,1},... | collective-permute-start | bytes 3145736 | tf_op jit(solution)/shard_map/ppermute | solution.py:68
  53.3 1.9 %collective-permute-start.5 = (bf16[256,1024]{1,0:T(8,128)(2,1)S(1)}, bf16[256,1024]{1,0:T(8,128)(2,1)}, u32[]{:S(2)}, u32[]{:S(2)}) collective-permute-start(bf16[256,1024]{1,0:T(8,128)(2,1)S(1)} %copy-done.5), channel_id=1, source_target_pairs={{0,20},{1,21},{2,22},{3,23},{4,16},{5,17},{6,18},{7,19},{8,28},{9,... | collective-permute-start | bytes 1572872 | tf_op jit(solution)/shard_map/ppermute | solution.py:68
  55.3 3.2 %collective-permute-start.6 = (bf16[256,1024]{1,0:T(8,128)(2,1)}, bf16[256,1024]{1,0:T(8,128)(2,1)}, u32[]{:S(2)}, u32[]{:S(2)}) collective-permute-start(bf16[256,1024]{1,0:T(8,128)(2,1)} %collective-permute-done.2), channel_id=1, source_target_pairs={{0,1},{1,0},{2,3},{3,2},{4,5},{5,4},{6,7},{7,6},{8,9},{9,8},{10,11... | collective-permute-start | bytes 1572872 | tf_op jit(solution)/shard_map/ppermute | solution.py:68
  58.4 11.1 %collective-permute-done.5.mh = bf16[256,1024]{1,0:T(8,128)(2,1)} collective-permute-done((bf16[256,1024]{1,0:T(8,128)(2,1)S(1)}, bf16[256,1024]{1,0:T(8,128)(2,1)}, u32[]{:S(2)}, u32[]{:S(2)}) %collective-permute-start.5) | collective-permute-done | bytes 524320 | tf_op jit(solution)/shard_map/ppermute | solution.py:68
  69.5 3.3 %collective-permute-start.12 = (bf16[256,1024]{1,0:T(8,128)(2,1)}, bf16[256,1024]{1,0:T(8,128)(2,1)}, u32[]{:S(2)}, u32[]{:S(2)}) collective-permute-start(bf16[256,1024]{1,0:T(8,128)(2,1)} %collective-permute-done.5.mh), channel_id=1, source_target_pairs={{0,8},{1,9},{2,10},{3,11},{4,12},{5,13},{6,14},{7,15},{8,0},{9,1},... | collective-permute-start | bytes 1572872 | tf_op jit(solution)/shard_map/ppermute | solution.py:68
  72.8 14.3 %collective-permute-start.7 = (bf16[4,4,16,1024]{3,2,1,0:T(8,128)(2,1)}, bf16[4,4,16,1024]{3,2,1,0:T(8,128)(2,1)}, u32[]{:S(2)}, u32[]{:S(2)}) collective-permute-start(bf16[4,4,16,1024]{3,2,1,0:T(8,128)(2,1)} %bitcast.14.here), channel_id=1, source_target_pairs={{0,480},{1,481},{2,482},{3,483},{4,484},{5,485},{6,486},{7,487},{8... | collective-permute-start | bytes 1572872 | tf_op jit(solution)/shard_map/ppermute | solution.py:68
  87.1 1.9 %collective-permute-start.8 = (bf16[4,4,16,1024]{3,2,1,0:T(8,128)(2,1)}, bf16[4,4,16,1024]{3,2,1,0:T(8,128)(2,1)}, u32[]{:S(2)}, u32[]{:S(2)}) collective-permute-start(bf16[4,4,16,1024]{3,2,1,0:T(8,128)(2,1)} %bitcast.14.here), channel_id=1, source_target_pairs={{0,448},{1,449},{2,450},{3,451},{4,452},{5,453},{6,454},{7,455},{8... | collective-permute-start | bytes 1572872 | tf_op jit(solution)/shard_map/ppermute | solution.py:68
  89.0 1.9 %collective-permute-start.9 = (bf16[4,4,16,1024]{3,2,1,0:T(8,128)(2,1)}, bf16[4,4,16,1024]{3,2,1,0:T(8,128)(2,1)}, u32[]{:S(2)}, u32[]{:S(2)}) collective-permute-start(bf16[4,4,16,1024]{3,2,1,0:T(8,128)(2,1)} %bitcast.14.here), channel_id=1, source_target_pairs={{0,32},{1,33},{2,34},{3,35},{4,36},{5,37},{6,38},{7,39},{8,40},{9,... | collective-permute-start | bytes 1572872 | tf_op jit(solution)/shard_map/ppermute | solution.py:68
  91.0 3.7 %collective-permute-start.13 = (bf16[256,1024]{1,0:T(8,128)(2,1)}, bf16[256,1024]{1,0:T(8,128)(2,1)}, u32[]{:S(2)}, u32[]{:S(2)}) collective-permute-start(bf16[256,1024]{1,0:T(8,128)(2,1)} %collective-permute-done.6.mg), channel_id=1, source_target_pairs={{0,8},{1,9},{2,10},{3,11},{4,12},{5,13},{6,14},{7,15},{8,0},{9,1},... | collective-permute-start | bytes 1572872 | tf_op jit(solution)/shard_map/ppermute | solution.py:68
  94.7 9.5 %collective-permute-done.7.up = bf16[4,4,16,1024]{3,2,1,0:T(8,128)(2,1)} collective-permute-done((bf16[4,4,16,1024]{3,2,1,0:T(8,128)(2,1)}, bf16[4,4,16,1024]{3,2,1,0:T(8,128)(2,1)}, u32[]{:S(2)}, u32[]{:S(2)}) %collective-permute-start.7) | collective-permute-done | bytes 524320 | tf_op jit(solution)/shard_map/ppermute | solution.py:68
  104.2 4.2 %collective-permute-done.8.two = bf16[4,4,16,1024]{3,2,1,0:T(8,128)(2,1)} collective-permute-done((bf16[4,4,16,1024]{3,2,1,0:T(8,128)(2,1)}, bf16[4,4,16,1024]{3,2,1,0:T(8,128)(2,1)}, u32[]{:S(2)}, u32[]{:S(2)}) %collective-permute-start.8) | collective-permute-done | bytes 524320 | tf_op jit(solution)/shard_map/ppermute | solution.py:68
  108.5 4.3 %collective-permute-done.9.down = bf16[4,4,16,1024]{3,2,1,0:T(8,128)(2,1)} collective-permute-done((bf16[4,4,16,1024]{3,2,1,0:T(8,128)(2,1)}, bf16[4,4,16,1024]{3,2,1,0:T(8,128)(2,1)}, u32[]{:S(2)}, u32[]{:S(2)}) %collective-permute-start.9) | collective-permute-done | bytes 524320 | tf_op jit(solution)/shard_map/ppermute | solution.py:68
  112.8 4.8 %own_products.1 = (f32[4,8,72,128]{3,2,1,0:T(8,128)S(1)}, bf16[7,256,1024]{2,1,0:T(8,128)(2,1)S(1)}, bf16[4,256,1024]{2,1,0:T(8,128)(2,1)S(1)}) custom-call(s32[6]{0:T(128)S(1)} %stack.51.where, bf16[2,256,1024]{2,1,0:T(8,128)(2,1)S(1)} %pad_maximum_fusion.1.ma, bf16[4,256,1024]{2,1,0:T(8,128)(2,1)S(1)} %pad_maximum_fusion.mf, ...), custom_call_target="tpu_custom_call" | custom-call | tf_op jit(solution)/shard_map/own_products/pallas_call | solution.py:225
  117.6 3.7 %other_products.1 = f32[4,8,72,128]{3,2,1,0:T(8,128)S(1)} custom-call(s32[6]{0:T(128)S(1)} %stack.51.where, bf16[7,256,1024]{2,1,0:T(8,128)(2,1)S(1)} %get-tuple-element.6.xs, bf16[256,1024]{1,0:T(8,128)(2,1)} %collective-permute-done.13.ng, bf16[4,256,1024]{2,1,0:T(8,128)(2,1)S(1)} %get-tuple-element.7.kept, ...), custom_call_target="tpu_custom_call", output_to_operand_aliasing={{}: (4, {})} | custom-call | tf_op jit(solution)/shard_map/other_products/pallas_call | solution.py:242
  121.4 22.9 %all_to_all.10 = f32[32,72,128]{2,1,0:T(8,128)S(1)} all-to-all(f32[32,72,128]{2,1,0:T(8,128)S(1)} %bitcast.17), channel_id=1, replica_groups=mesh['zh'=4,'zl'=4,'yh'=2,'c'=2,'yl'=2,'xh'=2,'xl'=2] {'yh','c','yl','xh..., dimensions={0} | all-to-all | bytes 2359296 | tf_op jit(solution)/shard_map/all_to_all | solution.py:255
  (28 shorter events, 5.7 us)
Async XLA Ops:
  0.6 13.4 %collective-permute-start = (bf16[256,1024]{1,0:T(8,128)(2,1)}, bf16[256,1024]{1,0:T(8,128)(2,1)S(1)}, u32[]{:S(2)}, u32[]{:S(2)}) collective-permute-start(bf16[256,1024]{1,0:T(8,128)(2,1)} %orbitals.1), channel_id=1, source_target_pairs={{0,1},{1,0},{2,3},{3,2},{4,5},{5,4},{6,7},{7,6},{8,9},{9,8},{10,11... | collective-permute-start | bytes 1572872 | tf_op jit(solution)/shard_map/ppermute | solution.py:68
  4.6 33.7 %collective-permute-start.2 = (bf16[256,1024]{1,0:T(8,128)(2,1)}, bf16[256,1024]{1,0:T(8,128)(2,1)}, u32[]{:S(2)}, u32[]{:S(2)}) collective-permute-start(bf16[256,1024]{1,0:T(8,128)(2,1)} %orbitals.1), channel_id=1, source_target_pairs={{0,16},{1,17},{2,18},{3,19},{4,20},{5,21},{6,22},{7,23},{8,24},{9,... | collective-permute-start | bytes 1572872 | tf_op jit(solution)/shard_map/ppermute | solution.py:68
  9.4 28.9 %collective-permute-start.3 = (bf16[256,1024]{1,0:T(8,128)(2,1)}, bf16[256,1024]{1,0:T(8,128)(2,1)S(1)}, u32[]{:S(2)}, u32[]{:S(2)}) collective-permute-start(bf16[256,1024]{1,0:T(8,128)(2,1)} %orbitals.1), channel_id=1, source_target_pairs={{0,20},{1,21},{2,22},{3,23},{4,16},{5,17},{6,18},{7,19},{8,28},{9,... | collective-permute-start | bytes 1572872 | tf_op jit(solution)/shard_map/ppermute | solution.py:68
  12.1 26.2 %collective-permute-start.1 = (bf16[256,1024]{1,0:T(8,128)(2,1)}, bf16[256,1024]{1,0:T(8,128)(2,1)S(1)}, u32[]{:S(2)}, u32[]{:S(2)}) collective-permute-start(bf16[256,1024]{1,0:T(8,128)(2,1)} %orbitals.1), channel_id=1, source_target_pairs={{0,4},{1,5},{2,6},{3,7},{4,0},{5,1},{6,2},{7,3},{8,12},{9,13},{10,... | collective-permute-start | bytes 1572872 | tf_op jit(solution)/shard_map/ppermute | solution.py:68
  14.0 31.7 %copy-start.4 = (bf16[256,1024]{1,0:T(8,128)(2,1)}, bf16[256,1024]{1,0:T(8,128)(2,1)S(1)}, u32[]{:S(2)}) copy-start(bf16[256,1024]{1,0:T(8,128)(2,1)S(1)} %collective-permute-done) | copy-start | bytes 1572868
  14.1 30.0 %collective-permute-start.4 = (bf16[256,1024]{1,0:T(8,128)(2,1)S(1)}, bf16[256,1024]{1,0:T(8,128)(2,1)}, u32[]{:S(2)}, u32[]{:S(2)}) collective-permute-start(bf16[256,1024]{1,0:T(8,128)(2,1)S(1)} %collective-permute-done), channel_id=1, source_target_pairs={{0,4},{1,5},{2,6},{3,7},{4,0},{5,1},{6,2},{7,3},{8,12},{9,13},{10,... | collective-permute-start | bytes 1572872 | tf_op jit(solution)/shard_map/ppermute | solution.py:68
  19.7 1.0 copy-start
  20.7 0.7 copy-start.2
  22.4 50.4 %all-to-all-start = ((bf16[16,16,1024]{2,1,0:T(8,128)(2,1)}), bf16[16,16,1024]{2,1,0:T(8,128)(2,1)}, u32[]{:S(2)}, u32[]{:S(2)}) async-start(bf16[16,16,1024]{2,1,0:T(8,128)(2,1)} %bitcast.13), calls=%async_computation | async-start | bytes 1048576 | tf_op jit(solution)/shard_map/all_to_all | solution.py:193
  38.3 5.7 %copy-start.6 = (bf16[256,1024]{1,0:T(8,128)(2,1)}, bf16[256,1024]{1,0:T(8,128)(2,1)S(1)}, u32[]{:S(2)}) copy-start(bf16[256,1024]{1,0:T(8,128)(2,1)S(1)} %collective-permute-done.1) | copy-start | bytes 1572868
  44.0 6.1 %copy-start.1 = (bf16[256,1024]{1,0:T(8,128)(2,1)S(1)}, bf16[256,1024]{1,0:T(8,128)(2,1)}, u32[]{:S(2)}) copy-start(bf16[256,1024]{1,0:T(8,128)(2,1)} %orbitals.1) | copy-start | bytes 1572868
  45.7 67.1 %collective-permute-start.11 = (bf16[4,256,1024]{2,1,0:T(8,128)(2,1)S(1)}, bf16[4,256,1024]{2,1,0:T(8,128)(2,1)}, u32[]{:S(2)}, u32[]{:S(2)}) collective-permute-start(bf16[4,256,1024]{2,1,0:T(8,128)(2,1)S(1)} %pad_maximum_fusion.mf), channel_id=1, source_target_pairs={{0,8},{1,9},{2,10},{3,11},{4,12},{5,13},{6,14},{7,15},{8,0},{9,1},... | collective-permute-start | bytes 6291464 | tf_op jit(solution)/shard_map/ppermute | solution.py:68
  50.2 3.2 %copy-start.5 = (bf16[256,1024]{1,0:T(8,128)(2,1)S(1)}, bf16[256,1024]{1,0:T(8,128)(2,1)}, u32[]{:S(2)}) copy-start(bf16[256,1024]{1,0:T(8,128)(2,1)} %copy-done.4) | copy-start | bytes 1572868
  51.4 37.6 %collective-permute-start.10 = (bf16[2,256,1024]{2,1,0:T(8,128)(2,1)S(1)}, bf16[2,256,1024]{2,1,0:T(8,128)(2,1)}, u32[]{:S(2)}, u32[]{:S(2)}) collective-permute-start(bf16[2,256,1024]{2,1,0:T(8,128)(2,1)S(1)} %pad_maximum_fusion.1.ma), channel_id=1, source_target_pairs={{0,8},{1,9},{2,10},{3,11},{4,12},{5,13},{6,14},{7,15},{8,0},{9,1},... | collective-permute-start | bytes 3145736 | tf_op jit(solution)/shard_map/ppermute | solution.py:68
  53.3 16.2 %collective-permute-start.5 = (bf16[256,1024]{1,0:T(8,128)(2,1)S(1)}, bf16[256,1024]{1,0:T(8,128)(2,1)}, u32[]{:S(2)}, u32[]{:S(2)}) collective-permute-start(bf16[256,1024]{1,0:T(8,128)(2,1)S(1)} %copy-done.5), channel_id=1, source_target_pairs={{0,20},{1,21},{2,22},{3,23},{4,16},{5,17},{6,18},{7,19},{8,28},{9,... | collective-permute-start | bytes 1572872 | tf_op jit(solution)/shard_map/ppermute | solution.py:68
  55.3 31.8 %collective-permute-start.6 = (bf16[256,1024]{1,0:T(8,128)(2,1)}, bf16[256,1024]{1,0:T(8,128)(2,1)}, u32[]{:S(2)}, u32[]{:S(2)}) collective-permute-start(bf16[256,1024]{1,0:T(8,128)(2,1)} %collective-permute-done.2), channel_id=1, source_target_pairs={{0,1},{1,0},{2,3},{3,2},{4,5},{5,4},{6,7},{7,6},{8,9},{9,8},{10,11... | collective-permute-start | bytes 1572872 | tf_op jit(solution)/shard_map/ppermute | solution.py:68
  69.5 21.4 %collective-permute-start.12 = (bf16[256,1024]{1,0:T(8,128)(2,1)}, bf16[256,1024]{1,0:T(8,128)(2,1)}, u32[]{:S(2)}, u32[]{:S(2)}) collective-permute-start(bf16[256,1024]{1,0:T(8,128)(2,1)} %collective-permute-done.5.mh), channel_id=1, source_target_pairs={{0,8},{1,9},{2,10},{3,11},{4,12},{5,13},{6,14},{7,15},{8,0},{9,1},... | collective-permute-start | bytes 1572872 | tf_op jit(solution)/shard_map/ppermute | solution.py:68
  72.8 31.5 %collective-permute-start.7 = (bf16[4,4,16,1024]{3,2,1,0:T(8,128)(2,1)}, bf16[4,4,16,1024]{3,2,1,0:T(8,128)(2,1)}, u32[]{:S(2)}, u32[]{:S(2)}) collective-permute-start(bf16[4,4,16,1024]{3,2,1,0:T(8,128)(2,1)} %bitcast.14.here), channel_id=1, source_target_pairs={{0,480},{1,481},{2,482},{3,483},{4,484},{5,485},{6,486},{7,487},{8... | collective-permute-start | bytes 1572872 | tf_op jit(solution)/shard_map/ppermute | solution.py:68
  87.1 21.4 %collective-permute-start.8 = (bf16[4,4,16,1024]{3,2,1,0:T(8,128)(2,1)}, bf16[4,4,16,1024]{3,2,1,0:T(8,128)(2,1)}, u32[]{:S(2)}, u32[]{:S(2)}) collective-permute-start(bf16[4,4,16,1024]{3,2,1,0:T(8,128)(2,1)} %bitcast.14.here), channel_id=1, source_target_pairs={{0,448},{1,449},{2,450},{3,451},{4,452},{5,453},{6,454},{7,455},{8... | collective-permute-start | bytes 1572872 | tf_op jit(solution)/shard_map/ppermute | solution.py:68
  89.0 23.8 %collective-permute-start.9 = (bf16[4,4,16,1024]{3,2,1,0:T(8,128)(2,1)}, bf16[4,4,16,1024]{3,2,1,0:T(8,128)(2,1)}, u32[]{:S(2)}, u32[]{:S(2)}) collective-permute-start(bf16[4,4,16,1024]{3,2,1,0:T(8,128)(2,1)} %bitcast.14.here), channel_id=1, source_target_pairs={{0,32},{1,33},{2,34},{3,35},{4,36},{5,37},{6,38},{7,39},{8,40},{9,... | collective-permute-start | bytes 1572872 | tf_op jit(solution)/shard_map/ppermute | solution.py:68
  91.0 26.7 %collective-permute-start.13 = (bf16[256,1024]{1,0:T(8,128)(2,1)}, bf16[256,1024]{1,0:T(8,128)(2,1)}, u32[]{:S(2)}, u32[]{:S(2)}) collective-permute-start(bf16[256,1024]{1,0:T(8,128)(2,1)} %collective-permute-done.6.mg), channel_id=1, source_target_pairs={{0,8},{1,9},{2,10},{3,11},{4,12},{5,13},{6,14},{7,15},{8,0},{9,1},... | collective-permute-start | bytes 1572872 | tf_op jit(solution)/shard_map/ppermute | solution.py:68
  121.3 22.9 %copy-start.3 = (s32[64]{0:T(128)S(1)}, s32[64]{0:T(128)}, u32[]{:S(2)}) copy-start(s32[64]{0:T(128)} %points.1) | copy-start | bytes 772
